TPU v7x, 256 devices: a whole 4x4x8 slice. The times are simulated.
256 devices in a mesh: rx: 32 (over z, y_hi, core), tm: 8 (over y_lo, x).
Axes of the slice: x: 4, y: 4 (y_hi: 2, y_lo: 2; y = y_hi * 2 + y_lo), z: 8, core: 2. Of those that a mesh axis runs over, the one named last changes fastest.
Arguments:
- signals: float32 [2, 32, 524288], P(None, 'rx', 'tm'), may hold values from -6 to 6
Outputs:
- ambiguity: float32 [256, 2, 32, 4, 1, 256], P('tm', None, 'rx')
All inputs are finite; a program needn't handle non-finite values.
Results may differ from a plain program's by a relative error of at most 0.0003.
Values sent between devices are 32-bit elements; how exact they have to be, the bound alone decides.
A program may use at most 64 MiB of HBM per device.

v0:
```python
import math

import jax
import jax.numpy as jnp
from jax import lax
from jax.sharding import PartitionSpec as P

SEG_LEN = 4096
LAGS = 256
DOPLEN = 512
DOPK = 256
OFFS = 4


highest = lax.Precision.HIGHEST


def shifted(value, axis, steps):
    count = lax.axis_size(axis)
    pairs = [(source, (source + steps) % count) for source in range(count)]
    return lax.ppermute(value, axis, pairs)


def in_blocks(x, dim, size):
    before, after = (x.shape[:dim], x.shape[dim + 1 :])
    return jnp.moveaxis(x.reshape(*before, size, -1, *after), dim, 0)


def summed_on_arrival(x, axis, dim):
    size = lax.axis_size(axis)
    blocks = lax.all_to_all(in_blocks(x, dim, size), axis, 0, 0, tiled=True)
    return jnp.sum(blocks, axis=0)


def radix_tables(radix):
    index = jnp.arange(radix, dtype=jnp.int32)
    angle = 2.0 * math.pi / radix * (index[:, None] * index[None, :] % radix).astype(jnp.float32)
    return (jnp.cos(angle), -jnp.sin(angle))


def twiddle_tables(radix):
    length = radix * radix
    index = jnp.arange(radix, dtype=jnp.int32)
    angle = 2.0 * math.pi / length * (index[:, None] * index[None, :] % length).astype(jnp.float32)
    return (jnp.cos(angle), -jnp.sin(angle))


def forward(real_part, imag_part):
    rec_dev, length = (real_part.shape[0], real_part.shape[1])
    radix = math.isqrt(SEG_LEN)
    seg_dev = length // SEG_LEN
    shaped_re = real_part.reshape(rec_dev, seg_dev, radix, radix)
    shaped_im = imag_part.reshape(rec_dev, seg_dev, radix, radix)
    cos_a, sin_a = radix_tables(radix)
    first_re = jnp.einsum("ka,isab->sikb", cos_a, shaped_re, precision=highest) - jnp.einsum(
        "ka,isab->sikb", sin_a, shaped_im, precision=highest
    )
    first_im = jnp.einsum("ka,isab->sikb", cos_a, shaped_im, precision=highest) + jnp.einsum(
        "ka,isab->sikb", sin_a, shaped_re, precision=highest
    )
    twist_re, twist_im = twiddle_tables(radix)
    turned_re = first_re * twist_re - first_im * twist_im
    turned_im = first_re * twist_im + first_im * twist_re
    second_re = jnp.einsum("sikb,bc->sikc", turned_re, cos_a, precision=highest) - jnp.einsum(
        "sikb,bc->sikc", turned_im, sin_a, precision=highest
    )
    second_im = jnp.einsum("sikb,bc->sikc", turned_re, sin_a, precision=highest) + jnp.einsum(
        "sikb,bc->sikc", turned_im, cos_a, precision=highest
    )
    return jnp.stack(
        [second_re.reshape(seg_dev, rec_dev, SEG_LEN), second_im.reshape(seg_dev, rec_dev, SEG_LEN)]
    )


def lag_table(length, lags):
    radix = math.isqrt(length)
    position = jnp.arange(length, dtype=jnp.int32)
    frequency = position // radix + radix * (position % radix)
    offset = jnp.arange(lags, dtype=jnp.int32) - lags // 2
    angle = (
        2.0 * math.pi / length * (frequency[:, None] * offset[None, :] % length).astype(jnp.float32)
    )
    return jnp.concatenate([jnp.cos(angle), jnp.sin(angle)], axis=1) / length


def doppler_tables(first_seg, count):
    segment = first_seg + jnp.arange(count, dtype=jnp.int32)
    frequency = jnp.arange(DOPK, dtype=jnp.int32) - DOPK // 2
    angle = (
        2.0
        * math.pi
        / DOPLEN
        * (segment[:, None] * frequency[None, :] % DOPLEN).astype(jnp.float32)
    )
    return (jnp.cos(angle), -jnp.sin(angle))


def correlate_all(own, partners, table):
    own_re, own_im = (own[0][None, :, :, None, :], own[1][None, :, :, None, :])
    far_stack = jnp.stack(partners)
    far_re, far_im = (far_stack[:, 0][:, :, None, :, :], far_stack[:, 1][:, :, None, :, :])
    prod_re = own_re * far_re + own_im * far_im
    prod_im = own_im * far_re - own_re * far_im
    shape = prod_re.shape[:-1] + (LAGS,)
    rows = prod_re.size // SEG_LEN
    stacked = jnp.concatenate(
        [prod_re.reshape(rows, SEG_LEN), prod_im.reshape(rows, SEG_LEN)], axis=0
    )
    mixed = jnp.dot(stacked, table, precision=highest)
    re_cos, re_sin = (mixed[:rows, :LAGS], mixed[:rows, LAGS:])
    im_cos, im_sin = (mixed[rows:, :LAGS], mixed[rows:, LAGS:])
    corr_re = (re_cos - im_sin).reshape(shape)
    corr_im = (re_sin + im_cos).reshape(shape)
    return (corr_re, corr_im)


def doppler(corr_re, corr_im, dop_cos, dop_sin):
    amb_re = jnp.einsum("sijl,sf->lijf", corr_re, dop_cos, precision=highest) - jnp.einsum(
        "sijl,sf->lijf", corr_im, dop_sin, precision=highest
    )
    amb_im = jnp.einsum("sijl,sf->lijf", corr_re, dop_sin, precision=highest) + jnp.einsum(
        "sijl,sf->lijf", corr_im, dop_cos, precision=highest
    )
    return jnp.stack([amb_re, amb_im], axis=1)


def per_device(signals):
    own = forward(signals[0], signals[1])
    seg_dev = own.shape[1]
    time_parts = lax.axis_size("tm")
    total_segs = seg_dev * time_parts
    table = lag_table(SEG_LEN, LAGS)
    scale = 1.0 / math.sqrt(2.0 * SEG_LEN * total_segs)
    dop_cos, dop_sin = doppler_tables(lax.axis_index("tm") * seg_dev, seg_dev)
    far = own
    partners = []
    for step in range(1, OFFS + 1):
        far = shifted(own, "rx", step)
        partners.append(far)
    all_re, all_im = correlate_all(own, partners, table)
    results = []
    for step in range(OFFS):
        corr_re = all_re[step]
        corr_im = all_im[step]

        def partial_term(start, count, corr_re=corr_re, corr_im=corr_im):
            return doppler(corr_re, corr_im, dop_cos, dop_sin)

        block = summed_on_arrival(
            partial_term(jnp.int32(0), LAGS // time_parts * lax.axis_size("tm")), "tm", 0
        )
        results.append(block * scale)
    return jnp.stack(results, axis=3)


def solution(mesh):
    return jax.shard_map(
        per_device,
        mesh=mesh,
        in_specs=(P(None, "rx", "tm"),),
        out_specs=P("tm", None, "rx", None, None, None),
        check_vma=False,
    )
```

profile of v0, /device:TPU:16, one launch (start us, length us, event | category | flops | bytes accessed | tf_op | source)
XLA Modules:
  0.0 123.6 jit_solution(18164984450579093374)
XLA Ops:
  0.1 2.4 %slice_reduce_fusion.1 = (f32[65536]{0:T(1024)S(1)}, f32[65536]{0:T(1024)S(1)}) fusion(f32[2,1,65536]{2,1,0:T(1,128)} %param.1), kind=kLoop, calls=%fused_computation.53 | loop fusion | bytes 1048576 | tf_op jit(solution)/shard_map/slice | solution.py:128
  2.7 0.7 fusion.32
  3.6 0.7 fusion.34
  4.3 0.7 fusion.12
  5.0 0.7 fusion.13
  6.5 0.7 fusion.20
  7.2 0.7 convolution_add_fusion
  9.0 0.7 constant_dynamic-update-slice_fusion.1
  9.8 0.7 constant_dynamic-update-slice_fusion
  10.5 1.7 %collective-permute-start.1 = (f32[2,16,1,4096]{3,1,0,2:T(8,128)}, f32[2,16,1,4096]{3,1,0,2:T(8,128)S(1)}, u32[]{:S(2)}, u32[]{:S(2)}) collective-permute-start(f32[2,16,1,4096]{3,1,0,2:T(8,128)} %bitcast.15), channel_id=1, source_target_pairs={{0,16},{8,24},{16,32},{24,40},{32,48},{40,56},{48,64},{56,72},{64,... | collective-permute-start | bytes 1572872 | tf_op jit(solution)/shard_map/ppermute | solution.py:21
  12.2 4.3 %collective-permute-start.2 = (f32[2,16,1,4096]{3,1,0,2:T(8,128)}, f32[2,16,1,4096]{3,1,0,2:T(8,128)S(1)}, u32[]{:S(2)}, u32[]{:S(2)}) collective-permute-start(f32[2,16,1,4096]{3,1,0,2:T(8,128)} %bitcast.15), channel_id=1, source_target_pairs={{0,24},{8,32},{16,40},{24,48},{32,56},{40,64},{48,72},{56,80},{64,... | collective-permute-start | bytes 1572872 | tf_op jit(solution)/shard_map/ppermute | solution.py:21
  16.5 1.9 %collective-permute-start.3 = (f32[2,16,1,4096]{3,1,2,0:T(8,128)}, f32[2,16,1,4096]{3,1,2,0:T(8,128)}, u32[]{:S(2)}, u32[]{:S(2)}) collective-permute-start(f32[2,16,1,4096]{3,1,2,0:T(8,128)} %constant_dynamic-update-slice_fusion), channel_id=1, source_target_pairs={{0,32},{8,40},{16,48},{24,56},{32,64},{40,72},{48,80},{56,88},{64,... | collective-permute-start | bytes 1572872 | tf_op jit(solution)/shard_map/ppermute | solution.py:21
  18.4 18.9 %fusion.11 = (f32[4096,256]{1,0:T(8,128)}, f32[4096,256]{1,0:T(8,128)}) fusion(s32[256]{0:T(256)S(1)} %iota_add_fusion, s32[4096]{0:T(1024)S(1)} %fusion.51), kind=kLoop, calls=%fused_computation.18 | loop fusion | flops 14680064 | bytes 8406016 | tf_op jit(solution)/shard_map/cos | solution.py:83
  37.8 12.3 %collective-permute-done.2 = f32[2,16,1,4096]{3,1,0,2:T(8,128)S(1)} collective-permute-done((f32[2,16,1,4096]{3,1,0,2:T(8,128)}, f32[2,16,1,4096]{3,1,0,2:T(8,128)S(1)}, u32[]{:S(2)}, u32[]{:S(2)}) %collective-permute-start.2) | collective-permute-done | bytes 524320 | tf_op jit(solution)/shard_map/ppermute | solution.py:21
  50.1 1.8 %collective-permute-done.3 = f32[2,16,1,4096]{3,1,2,0:T(8,128)} collective-permute-done((f32[2,16,1,4096]{3,1,2,0:T(8,128)}, f32[2,16,1,4096]{3,1,2,0:T(8,128)}, u32[]{:S(2)}, u32[]{:S(2)}) %collective-permute-start.3) | collective-permute-done | bytes 524320 | tf_op jit(solution)/shard_map/ppermute | solution.py:21
  51.9 1.2 pad_maximum_fusion
  53.6 1.7 %copy-done = f32[4096,256]{1,0:T(8,128)S(1)} copy-done((f32[4096,256]{1,0:T(8,128)S(1)}, f32[4096,256]{1,0:T(8,128)}, u32[]{:S(2)}) %copy-start) | copy-done | bytes 4194328
  55.3 1.3 %copy-done.1 = f32[4096,256]{1,0:T(8,128)S(1)} copy-done((f32[4096,256]{1,0:T(8,128)S(1)}, f32[4096,256]{1,0:T(8,128)}, u32[]{:S(2)}) %copy-start.1) | copy-done | bytes 4194328
  56.6 4.9 %fusion = f32[128,512]{1,0:T(8,128)S(1)} fusion(f32[4096,256]{1,0:T(8,128)S(1)} %copy-done.1, f32[4096,256]{1,0:T(8,128)S(1)} %copy-done, f32[64,4096]{1,0:T(8,128)S(1)} %get-tuple-element.8, f32[64,4096]{1,0:T(8,128)S(1)} %get-tuple-element.7), kind=kOutput, calls=%fused_computation.1 | convolution fusion | flops 3225944064 | bytes 10747904 | tf_op jit(solution)/shard_map/dot_general | solution.py:109
  65.6 0.8 pad_maximum_fusion.1
  66.4 5.0 %all-to-all-start = ((f32[8,32,2,1,1,256]{5,1,4,3,2,0:T(8,128)}), f32[8,32,2,1,1,256]{5,1,4,3,2,0:T(8,128)S(1)}, u32[]{:S(2)}, u32[]{:S(2)}) async-start(f32[8,32,2,1,1,256]{5,1,4,3,2,0:T(8,128)} %pad_maximum_fusion.1), calls=%async_computation | async-start | bytes 1048576 | tf_op jit(solution)/shard_map/all_to_all | solution.py:31
  73.0 0.8 pad_maximum_fusion.2
  74.3 0.8 pad_maximum_fusion.3
  75.1 5.0 %all-to-all-done = f32[8,32,2,1,1,256]{5,1,4,3,2,0:T(8,128)S(1)} async-done(((f32[8,32,2,1,1,256]{5,1,4,3,2,0:T(8,128)}), f32[8,32,2,1,1,256]{5,1,4,3,2,0:T(8,128)S(1)}, u32[]{:S(2)}, u32[]{:S(2)}) %all-to-all-start) | async-done | bytes 524320 | tf_op jit(solution)/shard_map/all_to_all | solution.py:31
  80.1 3.5 %all-to-all-start.1 = ((f32[8,32,2,1,1,256]{5,1,4,3,2,0:T(8,128)}), f32[8,32,2,1,1,256]{5,1,4,3,2,0:T(8,128)S(1)}, u32[]{:S(2)}, u32[]{:S(2)}) async-start(f32[8,32,2,1,1,256]{5,1,4,3,2,0:T(8,128)} %pad_maximum_fusion.2), calls=%async_computation.1 | async-start | bytes 1048576 | tf_op jit(solution)/shard_map/all_to_all | solution.py:31
  84.6 9.6 %all-to-all-done.1 = f32[8,32,2,1,1,256]{5,1,4,3,2,0:T(8,128)S(1)} async-done(((f32[8,32,2,1,1,256]{5,1,4,3,2,0:T(8,128)}), f32[8,32,2,1,1,256]{5,1,4,3,2,0:T(8,128)S(1)}, u32[]{:S(2)}, u32[]{:S(2)}) %all-to-all-start.1) | async-done | bytes 524320 | tf_op jit(solution)/shard_map/all_to_all | solution.py:31
  94.3 3.5 %all-to-all-start.2 = ((f32[8,32,2,1,1,256]{5,1,4,3,2,0:T(8,128)}), f32[8,32,2,1,1,256]{5,1,4,3,2,0:T(8,128)S(1)}, u32[]{:S(2)}, u32[]{:S(2)}) async-start(f32[8,32,2,1,1,256]{5,1,4,3,2,0:T(8,128)} %pad_maximum_fusion.3), calls=%async_computation.2 | async-start | bytes 1048576 | tf_op jit(solution)/shard_map/all_to_all | solution.py:31
  98.8 0.8 pad_maximum_fusion.4
  99.6 9.2 %all-to-all-done.2 = f32[8,32,2,1,1,256]{5,1,4,3,2,0:T(8,128)S(1)} async-done(((f32[8,32,2,1,1,256]{5,1,4,3,2,0:T(8,128)}), f32[8,32,2,1,1,256]{5,1,4,3,2,0:T(8,128)S(1)}, u32[]{:S(2)}, u32[]{:S(2)}) %all-to-all-start.2) | async-done | bytes 524320 | tf_op jit(solution)/shard_map/all_to_all | solution.py:31
  108.8 3.5 %all-to-all-start.3 = ((f32[8,32,2,1,1,256]{5,1,4,3,2,0:T(8,128)}), f32[8,32,2,1,1,256]{5,1,4,3,2,0:T(8,128)S(1)}, u32[]{:S(2)}, u32[]{:S(2)}) async-start(f32[8,32,2,1,1,256]{5,1,4,3,2,0:T(8,128)} %pad_maximum_fusion.4), calls=%async_computation.3 | async-start | bytes 1048576 | tf_op jit(solution)/shard_map/all_to_all | solution.py:31
  112.5 10.1 %all-to-all-done.3 = f32[8,32,2,1,1,256]{5,1,4,3,2,0:T(8,128)S(1)} async-done(((f32[8,32,2,1,1,256]{5,1,4,3,2,0:T(8,128)}), f32[8,32,2,1,1,256]{5,1,4,3,2,0:T(8,128)S(1)}, u32[]{:S(2)}, u32[]{:S(2)}) %all-to-all-start.3) | async-done | bytes 524320 | tf_op jit(solution)/shard_map/all_to_all | solution.py:31
  122.6 1.0 copy.23
  (45 shorter events, 11.3 us)
Async XLA Ops:
  10.5 27.3 %collective-permute-start = (f32[2,16,1,4096]{3,1,0,2:T(8,128)}, f32[2,16,1,4096]{3,1,0,2:T(8,128)S(1)}, u32[]{:S(2)}, u32[]{:S(2)}) collective-permute-start(f32[2,16,1,4096]{3,1,0,2:T(8,128)} %bitcast.15), channel_id=1, source_target_pairs={{0,8},{8,16},{16,24},{24,32},{32,40},{40,48},{48,56},{56,64},{64,7... | collective-permute-start | bytes 1572872 | tf_op jit(solution)/shard_map/ppermute | solution.py:21
  10.5 27.3 %collective-permute-start.1 = (f32[2,16,1,4096]{3,1,0,2:T(8,128)}, f32[2,16,1,4096]{3,1,0,2:T(8,128)S(1)}, u32[]{:S(2)}, u32[]{:S(2)}) collective-permute-start(f32[2,16,1,4096]{3,1,0,2:T(8,128)} %bitcast.15), channel_id=1, source_target_pairs={{0,16},{8,24},{16,32},{24,40},{32,48},{40,56},{48,64},{56,72},{64,... | collective-permute-start | bytes 1572872 | tf_op jit(solution)/shard_map/ppermute | solution.py:21
  12.2 37.9 %collective-permute-start.2 = (f32[2,16,1,4096]{3,1,0,2:T(8,128)}, f32[2,16,1,4096]{3,1,0,2:T(8,128)S(1)}, u32[]{:S(2)}, u32[]{:S(2)}) collective-permute-start(f32[2,16,1,4096]{3,1,0,2:T(8,128)} %bitcast.15), channel_id=1, source_target_pairs={{0,24},{8,32},{16,40},{24,48},{32,56},{40,64},{48,72},{56,80},{64,... | collective-permute-start | bytes 1572872 | tf_op jit(solution)/shard_map/ppermute | solution.py:21
  16.5 35.4 %collective-permute-start.3 = (f32[2,16,1,4096]{3,1,2,0:T(8,128)}, f32[2,16,1,4096]{3,1,2,0:T(8,128)}, u32[]{:S(2)}, u32[]{:S(2)}) collective-permute-start(f32[2,16,1,4096]{3,1,2,0:T(8,128)} %constant_dynamic-update-slice_fusion), channel_id=1, source_target_pairs={{0,32},{8,40},{16,48},{24,56},{32,64},{40,72},{48,80},{56,88},{64,... | collective-permute-start | bytes 1572872 | tf_op jit(solution)/shard_map/ppermute | solution.py:21
  53.1 2.2 %copy-start = (f32[4096,256]{1,0:T(8,128)S(1)}, f32[4096,256]{1,0:T(8,128)}, u32[]{:S(2)}) copy-start(f32[4096,256]{1,0:T(8,128)} %get-tuple-element.13) | copy-start | bytes 12582916
  53.1 3.5 %copy-start.1 = (f32[4096,256]{1,0:T(8,128)S(1)}, f32[4096,256]{1,0:T(8,128)}, u32[]{:S(2)}) copy-start(f32[4096,256]{1,0:T(8,128)} %get-tuple-element.14) | copy-start | bytes 12582916
  66.4 13.7 %all-to-all-start = ((f32[8,32,2,1,1,256]{5,1,4,3,2,0:T(8,128)}), f32[8,32,2,1,1,256]{5,1,4,3,2,0:T(8,128)S(1)}, u32[]{:S(2)}, u32[]{:S(2)}) async-start(f32[8,32,2,1,1,256]{5,1,4,3,2,0:T(8,128)} %pad_maximum_fusion.1), calls=%async_computation | async-start | bytes 1048576 | tf_op jit(solution)/shard_map/all_to_all | solution.py:31
  80.1 14.2 %all-to-all-start.1 = ((f32[8,32,2,1,1,256]{5,1,4,3,2,0:T(8,128)}), f32[8,32,2,1,1,256]{5,1,4,3,2,0:T(8,128)S(1)}, u32[]{:S(2)}, u32[]{:S(2)}) async-start(f32[8,32,2,1,1,256]{5,1,4,3,2,0:T(8,128)} %pad_maximum_fusion.2), calls=%async_computation.1 | async-start | bytes 1048576 | tf_op jit(solution)/shard_map/all_to_all | solution.py:31
  94.3 14.6 %all-to-all-start.2 = ((f32[8,32,2,1,1,256]{5,1,4,3,2,0:T(8,128)}), f32[8,32,2,1,1,256]{5,1,4,3,2,0:T(8,128)S(1)}, u32[]{:S(2)}, u32[]{:S(2)}) async-start(f32[8,32,2,1,1,256]{5,1,4,3,2,0:T(8,128)} %pad_maximum_fusion.3), calls=%async_computation.2 | async-start | bytes 1048576 | tf_op jit(solution)/shard_map/all_to_all | solution.py:31
  108.8 13.7 %all-to-all-start.3 = ((f32[8,32,2,1,1,256]{5,1,4,3,2,0:T(8,128)}), f32[8,32,2,1,1,256]{5,1,4,3,2,0:T(8,128)S(1)}, u32[]{:S(2)}, u32[]{:S(2)}) async-start(f32[8,32,2,1,1,256]{5,1,4,3,2,0:T(8,128)} %pad_maximum_fusion.4), calls=%async_computation.3 | async-start | bytes 1048576 | tf_op jit(solution)/shard_map/all_to_all | solution.py:31
where the time goes:
time: 124 us
  waiting for transfers between devices  48 us (39%)
  other arithmetic  24.1 us (19%)
  starting transfers between devices  23.4 us (19%)
  matrix products  18.6 us (15%)
  local copies, waits for them, and re-layouts  9.06 us (7%)
    all_to_all x4, waiting for transfers between devices, summed_on_arrival(): blocks = lax.all_to_all(in_blocks(x, dim, size), axis, 0, 0, tiled=True)  33.9 us
    cos x1, other arithmetic, lag_table(): return jnp.concatenate([jnp.cos(angle), jnp.sin(angle)], axis=1) / length  18.9 us
    all_to_all x4, starting transfers between devices, summed_on_arrival(): blocks = lax.all_to_all(in_blocks(x, dim, size), axis, 0, 0, tiled=True)  15.5 us
    ppermute x4, waiting for transfers between devices, shifted(): return lax.ppermute(value, axis, pairs)  14.1 us
    ppermute x4, starting transfers between devices, shifted(): return lax.ppermute(value, axis, pairs)  7.94 us
    dot_general x1, matrix products, correlate_all(): mixed = jnp.dot(stacked, table, precision=highest)  4.87 us
    unnamed x5, local copies, waits for them, and re-layouts  3.71 us
    another operation x4, other arithmetic, doppler(): return jnp.stack([amb_re, amb_im], axis=1)  3.34 us
  transfers between devices with their start and end apart: 8, of which 6 were waited for; matrix products, arithmetic and copies ran while one was open for 21% of the time, Pallas kernels for 0%

commit v1 on v0

v1 whole, which is shorter than its diff:
```python
import math

import jax
import jax.numpy as jnp
import numpy as np
from jax import lax
from jax.sharding import PartitionSpec as P

SEG_LEN = 4096
LAGS = 256
DOPLEN = 512
DOPK = 256
OFFS = 4
BLOCK = 256
WINDOW = 512

PRECISION = lax.Precision.HIGH


def forward_table():
    sample = np.arange(WINDOW)[:, None]
    freq = np.arange(WINDOW // 2)[None, :] + 0.5
    angle = 2.0 * np.pi / WINDOW * sample * freq
    return np.concatenate([np.cos(angle), np.sin(angle)], axis=1).astype(np.float32)


def inverse_table():
    lag = np.arange(LAGS)[None, :]
    freq = np.arange(WINDOW // 2)[:, None] + 0.5
    angle = 2.0 * np.pi / WINDOW * lag * freq
    return (np.concatenate([np.cos(angle), np.sin(angle)], axis=0) / WINDOW).astype(np.float32)


def doppler_table(segs):
    seg = np.arange(segs)[:, None]
    freq = np.arange(DOPK)[None, :] - DOPK // 2
    angle = 2.0 * np.pi / DOPLEN * (seg * freq % DOPLEN)
    scale = 1.0 / math.sqrt(2.0 * SEG_LEN * segs)
    cos, sin = np.cos(angle) * scale, -np.sin(angle) * scale
    return np.concatenate(
        [np.concatenate([cos, sin], axis=1), np.concatenate([-sin, cos], axis=1)], axis=0
    ).astype(np.float32)


def shifted(value, axis, steps):
    count = lax.axis_size(axis)
    pairs = [(source, (source + steps) % count) for source in range(count)]
    return lax.ppermute(value, axis, pairs)


def spectra(rows, table):
    half = WINDOW // 2
    mixed = jnp.dot(rows, table, precision=PRECISION)
    a_cos, a_sin = mixed[0, ..., :half], mixed[0, ..., half:]
    b_cos, b_sin = mixed[1, ..., :half], mixed[1, ..., half:]
    return a_cos + b_sin, b_cos - a_sin, a_cos - b_sin, b_cos + a_sin


def per_device(signals):
    seg_dev = signals.shape[2] // SEG_LEN
    parts = lax.axis_size("tm")
    x = signals.reshape(2, seg_dev, SEG_LEN // BLOCK, BLOCK)
    fars = jnp.stack([shifted(signals, "rx", step) for step in range(1, OFFS + 1)], axis=1)
    fars = fars.reshape(2, OFFS, seg_dev, SEG_LEN // BLOCK, BLOCK)
    half = BLOCK // 2
    table = jnp.asarray(forward_table())
    before = jnp.roll(x, 1, axis=2)[..., half:]
    after = jnp.roll(x, -1, axis=2)[..., :half]
    window = jnp.concatenate([before, x, after], axis=3)
    q = [v[None] for v in spectra(window, table)]
    p = spectra(fars, table[:BLOCK])
    pos_re = jnp.sum(q[0] * p[0] + q[1] * p[1], axis=2)
    pos_im = jnp.sum(q[1] * p[0] - q[0] * p[1], axis=2)
    neg_re = jnp.sum(q[2] * p[2] + q[3] * p[3], axis=2)
    neg_im = jnp.sum(q[3] * p[2] - q[2] * p[3], axis=2)
    even = jnp.concatenate([pos_re + neg_re, neg_im - pos_im], axis=2)
    odd = jnp.concatenate([pos_im + neg_im, pos_re - neg_re], axis=2)
    corr = jnp.dot(jnp.stack([even, odd]), jnp.asarray(inverse_table()), precision=PRECISION)
    blocks = jnp.moveaxis(corr.reshape(2, OFFS, seg_dev, parts, LAGS // parts), 3, 0)
    mine = lax.all_to_all(blocks, "tm", 0, 0, tiled=True)
    segs = parts * seg_dev
    rows = jnp.transpose(mine, (4, 2, 1, 0, 3)).reshape(LAGS // parts, OFFS, 2 * segs)
    out = jnp.dot(rows, jnp.asarray(doppler_table(segs)), precision=PRECISION)
    out = out.reshape(LAGS // parts, OFFS, 2, DOPK)
    return jnp.transpose(out, (0, 2, 1, 3))[:, :, None, :, None, :]


def solution(mesh):
    return jax.shard_map(
        per_device,
        mesh=mesh,
        in_specs=(P(None, "rx", "tm"),),
        out_specs=P("tm", None, "rx", None, None, None),
        check_vma=False,
    )
```

time: 124 us -> 68.3 us (0.55)
  the two profiles are of different devices: /device:TPU:16 before, /device:TPU:17 now
where the time goes in v1:
time: 68.3 us; the launch traced here: 68 us
  waiting for transfers between devices  29.7 us (43%)
  other arithmetic  13.8 us (20%)
  blocking collectives  9.97 us (15%)
  starting transfers between devices  6.53 us (10%)
  matrix products  5.22 us (8%)
  local copies, waits for them, and re-layouts  2.59 us (4%)
    ppermute x4, waiting for transfers between devices, shifted(): return lax.ppermute(value, axis, pairs)  29.7 us
    all_to_all x1, blocking collectives, per_device(): mine = lax.all_to_all(blocks, 'tm', 0, 0, tiled=True)  9.97 us
    ppermute x4, other arithmetic, shifted(): return lax.ppermute(value, axis, pairs)  8.45 us
    ppermute x4, starting transfers between devices, shifted(): return lax.ppermute(value, axis, pairs)  6.53 us
    dot_general x2, matrix products, spectra(): mixed = jnp.dot(rows, table, precision=PRECISION)  3.94 us
    unnamed x1, other arithmetic  2.57 us
    reduce_sum x1, other arithmetic, per_device(): neg_im = jnp.sum(q[3] * p[2] - q[2] * p[3], axis=2)  1.64 us
  transfers between devices with their start and end apart: 4, of which 4 were waited for; matrix products, arithmetic and copies ran while one was open for 15% of the time, Pallas kernels for 0%

profile of v1, /device:TPU:17, one launch (start us, length us, event | category | flops | bytes accessed | tf_op | source)
XLA Modules:
  0.0 68.0 jit_solution(534988941665098273)
XLA Ops:
  0.0 2.0 %collective-permute-start = (f32[2,1,65536]{2,1,0:T(1,128)}, f32[2,1,65536]{2,1,0:T(1,128)S(1)}, u32[]{:S(2)}, u32[]{:S(2)}) collective-permute-start(f32[2,1,65536]{2,1,0:T(1,128)} %param.4), channel_id=1, source_target_pairs={{0,8},{8,16},{16,24},{24,32},{32,40},{40,48},{48,56},{56,64},{64,7... | collective-permute-start | bytes 1572872 | tf_op jit(solution)/shard_map/ppermute | solution.py:48
  2.0 2.9 %collective-permute-start.1 = (f32[2,1,65536]{2,1,0:T(1,128)}, f32[2,1,65536]{2,1,0:T(1,128)S(1)}, u32[]{:S(2)}, u32[]{:S(2)}) collective-permute-start(f32[2,1,65536]{2,1,0:T(1,128)} %param.4), channel_id=1, source_target_pairs={{0,16},{8,24},{16,32},{24,40},{32,48},{40,56},{48,64},{56,72},{64,... | collective-permute-start | bytes 1572872 | tf_op jit(solution)/shard_map/ppermute | solution.py:48
  4.9 0.0 collective-permute-start.2
  4.9 1.6 %collective-permute-start.3 = (f32[2,1,65536]{2,1,0:T(1,128)}, f32[2,1,65536]{2,1,0:T(1,128)}, u32[]{:S(2)}, u32[]{:S(2)}) collective-permute-start(f32[2,1,65536]{2,1,0:T(1,128)} %param.4), channel_id=1, source_target_pairs={{0,32},{8,40},{16,48},{24,56},{32,64},{40,72},{48,80},{56,88},{64,... | collective-permute-start | bytes 1572872 | tf_op jit(solution)/shard_map/ppermute | solution.py:48
  6.5 2.6 %reduce = f32[2,65536]{1,0:T(2,128)S(1)} reduce(f32[2,1,65536]{2,1,0:T(1,128)} %param.4, f32[]{:T(128)} %constant.19), dimensions={1}, to_apply=%param.4.reduce_sub_computation | reduce | bytes 1048580 | tf_op args[0]
  9.1 0.1 fusion.32
  9.3 0.0 copy-done
  9.3 1.0 %fusion.9 = f32[2,16,16,512]{3,2,1,0:T(8,128)S(1)} fusion(f32[512,512,1,1]{1,0,3,2:T(8,128)S(1)} %copy-done, f32[2,16,1,256]{3,2,1,0:T(1,128)S(1)} %get-tuple-element.16, f32[2,16,15,256]{3,2,1,0:T(8,128)S(1)} %get-tuple-element.18, f32[2,16,15,256]{3,2,1,0:T(8,128)S(1)} %get-tuple-element.17, f32[2,16,1,256]{3,2,1,0:T(1,128)S(1)} %get-tuple-element.15, ...), kind=kOutput, calls=%fused_computation.11 | convolution fusion | flops 806354944 | bytes 3670016 | tf_op jit(solution)/shard_map/dot_general | solution.py:53
  10.3 0.1 subtract_bitcast_fusion
  10.5 2.9 %collective-permute-done = f32[2,1,65536]{2,1,0:T(1,128)S(1)} collective-permute-done((f32[2,1,65536]{2,1,0:T(1,128)}, f32[2,1,65536]{2,1,0:T(1,128)S(1)}, u32[]{:S(2)}, u32[]{:S(2)}) %collective-permute-start) | collective-permute-done | bytes 524320 | tf_op jit(solution)/shard_map/ppermute | solution.py:48
  13.4 1.7 %reduce.1 = f32[2,65536]{1,0:T(2,128)S(1)} reduce(f32[2,1,65536]{2,1,0:T(1,128)S(1)} %collective-permute-done, f32[]{:T(128)} %constant.19), dimensions={1}, to_apply=%ppermute.12.reduce_sub_computation | reduce | bytes 1048580 | tf_op jit(solution)/shard_map/ppermute | solution.py:48
  15.1 11.4 %collective-permute-done.1 = f32[2,1,65536]{2,1,0:T(1,128)S(1)} collective-permute-done((f32[2,1,65536]{2,1,0:T(1,128)}, f32[2,1,65536]{2,1,0:T(1,128)S(1)}, u32[]{:S(2)}, u32[]{:S(2)}) %collective-permute-start.1) | collective-permute-done | bytes 524320 | tf_op jit(solution)/shard_map/ppermute | solution.py:48
  26.5 1.7 %reduce.2 = f32[2,65536]{1,0:T(2,128)S(1)} reduce(f32[2,1,65536]{2,1,0:T(1,128)S(1)} %collective-permute-done.1, f32[]{:T(128)} %constant.19), dimensions={1}, to_apply=%ppermute.13.reduce_sub_computation | reduce | bytes 1048580 | tf_op jit(solution)/shard_map/ppermute | solution.py:48
  28.2 7.6 %collective-permute-done.2 = f32[2,1,65536]{2,1,0:T(1,128)} collective-permute-done((f32[2,1,65536]{2,1,0:T(1,128)}, f32[2,1,65536]{2,1,0:T(1,128)}, u32[]{:S(2)}, u32[]{:S(2)}) %collective-permute-start.2) | collective-permute-done | bytes 524320 | tf_op jit(solution)/shard_map/ppermute | solution.py:48
  35.9 2.6 %reduce.3 = f32[2,65536]{1,0:T(2,128)S(1)} reduce(f32[2,1,65536]{2,1,0:T(1,128)} %collective-permute-done.2, f32[]{:T(128)} %constant.19), dimensions={1}, to_apply=%ppermute.14.reduce_sub_computation | reduce | bytes 1048580 | tf_op jit(solution)/shard_map/ppermute | solution.py:48
  38.5 7.7 %collective-permute-done.3 = f32[2,1,65536]{2,1,0:T(1,128)} collective-permute-done((f32[2,1,65536]{2,1,0:T(1,128)}, f32[2,1,65536]{2,1,0:T(1,128)}, u32[]{:S(2)}, u32[]{:S(2)}) %collective-permute-start.3) | collective-permute-done | bytes 524320 | tf_op jit(solution)/shard_map/ppermute | solution.py:48
  46.2 2.6 %reduce.4 = f32[2,65536]{1,0:T(2,128)S(1)} reduce(f32[2,1,65536]{2,1,0:T(1,128)} %collective-permute-done.3, f32[]{:T(128)} %constant.19), dimensions={1}, to_apply=%ppermute.15.reduce_sub_computation | reduce | bytes 1048580 | tf_op jit(solution)/shard_map/ppermute | solution.py:48
  48.8 2.9 %fusion = f32[2,4,16,16,512]{4,3,2,1,0:T(8,128)S(1)} fusion(f32[256,512,1,1,1]{1,0,4,3,2:T(8,128)} %constant.16, f32[2,1,16,16,256]{4,3,2,1,0:T(8,128)S(1)} %bitcast.114, f32[2,1,16,16,256]{4,3,2,1,0:T(8,128)S(1)} %bitcast.113, f32[2,1,16,16,256]{4,3,2,1,0:T(8,128)S(1)} %bitcast.112, f32[2,1,16,16,256]{4,3,2,1,0:T(8,128)S(1)} %bitcast.111), kind=kOutput, calls=%fused_computation | convolution fusion | flops 1612185600 | bytes 6815744 | tf_op jit(solution)/shard_map/dot_general | solution.py:53
  51.7 0.0 copy-start.1
  51.7 1.6 %fusion.19 = (f32[4,16,256]{2,1,0:T(8,128)S(1)}, f32[4,16,256]{2,1,0:T(8,128)S(1)}, f32[4,16,256]{2,1,0:T(8,128)S(1)}, f32[4,16,256]{2,1,0:T(8,128)S(1)}) fusion(f32[16,16,256]{2,1,0:T(8,128)S(1)} %get-tuple-element.13, f32[16,16,256]{2,1,0:T(8,128)S(1)} %get-tuple-element.11, f32[2,4,16,16,512]{4,3,2,1,0:T(8,128)S(1)} %fusion, ...), kind=kLoop, calls=%fused_computation.22 | loop fusion | flops 5177344 | bytes 5505024 | tf_op jit(solution)/shard_map/reduce_sum | solution.py:75
  53.4 0.0 copy-done.1
  53.4 0.3 fusion.24
  53.7 0.2 reshape.25
  53.9 0.1 copy.28
  54.0 0.0 copy-start.2
  54.0 0.3 reshape.37
  54.3 10.0 %all_to_all.5 = f32[8,1,4096]{2,1,0:T(1,128)S(1)} all-to-all(f32[8,1,4096]{2,1,0:T(1,128)S(1)} %reshape.37), channel_id=1, replica_groups=mesh['rx'=32,'tm'=8] {'tm'}, dimensions={0} | all-to-all | bytes 262144 | tf_op jit(solution)/shard_map/all_to_all | solution.py:80
  64.2 0.5 broadcast.5
  64.8 1.0 %reduce.5 = f32[8,4096]{1,0:T(8,128)S(1)} reduce(f32[8,1,4096]{2,1,0:T(1,128)S(1)} %all_to_all.5, f32[]{:T(128)} %broadcast.5), dimensions={1}, to_apply=%all_to_all.3.reduce_sub_computation | reduce | bytes 262148 | tf_op jit(solution)/shard_map/all_to_all | solution.py:80
  65.7 0.2 reshape.38
  66.0 1.0 %convolution_bitcast_fusion = f32[32,2,1,4,1,256]{5,0,1,3,4,2:T(8,128)S(1)} fusion(f32[32,4,256,1]{0,2,3,1:T(8,128)S(1)} %bitcast.105, f32[2,256,256,1]{2,1,0,3:T(8,128)S(1)} %copy-done.2), kind=kOutput, calls=%fused_computation.8 | convolution fusion | flops 100663296 | bytes 917504 | tf_op jit(solution)/shard_map/dot_general | solution.py:83
  67.0 1.0 %copy.13 = f32[32,2,1,4,1,256]{5,4,3,2,1,0:T(1,128)} copy(f32[32,2,1,4,1,256]{5,0,1,3,4,2:T(8,128)S(1)} %convolution_bitcast_fusion) | data formatting | bytes 524288 | tf_op jit(solution)/shard_map/broadcast_in_dim | solution.py:85
  (13 shorter events, 0.4 us)
Async XLA Ops:
  0.0 9.3 %copy-start = (f32[512,512,1,1]{1,0,3,2:T(8,128)S(1)}, f32[512,512,1,1]{1,0,3,2:T(8,128)}, u32[]{:S(2)}) copy-start(f32[512,512,1,1]{1,0,3,2:T(8,128)} %constant.15) | copy-start | bytes 3145732
  0.0 13.4 %collective-permute-start = (f32[2,1,65536]{2,1,0:T(1,128)}, f32[2,1,65536]{2,1,0:T(1,128)S(1)}, u32[]{:S(2)}, u32[]{:S(2)}) collective-permute-start(f32[2,1,65536]{2,1,0:T(1,128)} %param.4), channel_id=1, source_target_pairs={{0,8},{8,16},{16,24},{24,32},{32,40},{40,48},{48,56},{56,64},{64,7... | collective-permute-start | bytes 1572872 | tf_op jit(solution)/shard_map/ppermute | solution.py:48
  2.0 24.5 %collective-permute-start.1 = (f32[2,1,65536]{2,1,0:T(1,128)}, f32[2,1,65536]{2,1,0:T(1,128)S(1)}, u32[]{:S(2)}, u32[]{:S(2)}) collective-permute-start(f32[2,1,65536]{2,1,0:T(1,128)} %param.4), channel_id=1, source_target_pairs={{0,16},{8,24},{16,32},{24,40},{32,48},{40,56},{48,64},{56,72},{64,... | collective-permute-start | bytes 1572872 | tf_op jit(solution)/shard_map/ppermute | solution.py:48
  4.9 31.0 %collective-permute-start.2 = (f32[2,1,65536]{2,1,0:T(1,128)}, f32[2,1,65536]{2,1,0:T(1,128)}, u32[]{:S(2)}, u32[]{:S(2)}) collective-permute-start(f32[2,1,65536]{2,1,0:T(1,128)} %param.4), channel_id=1, source_target_pairs={{0,24},{8,32},{16,40},{24,48},{32,56},{40,64},{48,72},{56,80},{64,... | collective-permute-start | bytes 1572872 | tf_op jit(solution)/shard_map/ppermute | solution.py:48
  4.9 41.3 %collective-permute-start.3 = (f32[2,1,65536]{2,1,0:T(1,128)}, f32[2,1,65536]{2,1,0:T(1,128)}, u32[]{:S(2)}, u32[]{:S(2)}) collective-permute-start(f32[2,1,65536]{2,1,0:T(1,128)} %param.4), channel_id=1, source_target_pairs={{0,32},{8,40},{16,48},{24,56},{32,64},{40,72},{48,80},{56,88},{64,... | collective-permute-start | bytes 1572872 | tf_op jit(solution)/shard_map/ppermute | solution.py:48
  51.7 1.7 %copy-start.1 = (f32[512,256,1,1]{1,0,3,2:T(8,128)S(1)}, f32[512,256,1,1]{1,0,3,2:T(8,128)}, u32[]{:S(2)}) copy-start(f32[512,256,1,1]{1,0,3,2:T(8,128)} %constant.17) | copy-start | bytes 1572868
  54.0 12.0 %copy-start.2 = (f32[2,256,256,1]{2,1,0,3:T(8,128)S(1)}, f32[2,256,256,1]{2,1,0,3:T(8,128)}, u32[]{:S(2)}) copy-start(f32[2,256,256,1]{2,1,0,3:T(8,128)} %constant.18) | copy-start | bytes 1572868

commit v2 on v1

v2 whole, which is shorter than its diff:
```python
import functools
import math

import jax
import jax.numpy as jnp
import ml_dtypes
import numpy as np
from jax import lax
from jax.experimental import pallas as pl
from jax.experimental.pallas import tpu as pltpu
from jax.sharding import PartitionSpec as P

SEG_LEN = 4096
LAGS = 256
DOPLEN = 512
DOPK = 256
OFFS = 4
WINDOW = 512
LANES = 128
GROUP = 4
SHARE = 4
UNITS = SEG_LEN // LANES
BLOCKS = SEG_LEN // 256
LAG_DEV = 32

MESH = pl.DeviceIdType.MESH

PAIRS = (
    ((0, 5), (1, 4)),
    ((0, 0), (1, 5), (2, 4)),
    ((0, 1), (1, 0), (2, 5), (3, 4)),
    ((0, 2), (1, 1), (2, 0), (3, 5)),
    ((2, 1), (3, 0)),
    ((3, 1),),
)


def split_table(table):
    table = table.astype(np.float32)
    high = table.astype(ml_dtypes.bfloat16)
    low = (table - high.astype(np.float32)).astype(ml_dtypes.bfloat16)
    return np.stack([high, low])


def forward_table():
    sample = np.arange(WINDOW)[:, None]
    freq = np.arange(WINDOW // 2)[None, :] + 0.5
    angle = 2.0 * np.pi / WINDOW * sample * freq
    return split_table(np.concatenate([np.cos(angle), np.sin(angle)], axis=1))


def inverse_table():
    lag = np.arange(LAGS)[None, :]
    freq = np.arange(WINDOW // 2)[:, None] + 0.5
    angle = 2.0 * np.pi / WINDOW * lag * freq
    return split_table(np.concatenate([np.cos(angle), np.sin(angle)], axis=0) / WINDOW)


def doppler_table(parts):
    seg = np.arange(parts * GROUP * SHARE).reshape(parts, GROUP, SHARE, 1)
    freq = np.arange(DOPK) - DOPK // 2
    angle = 2.0 * np.pi / DOPLEN * (seg * freq % DOPLEN)
    scale = 1.0 / math.sqrt(2.0 * SEG_LEN * parts * GROUP * SHARE)
    cos, sin = np.cos(angle) * scale, -np.sin(angle) * scale
    real_rows = np.concatenate([cos, sin], axis=-1)
    imag_rows = np.concatenate([-sin, cos], axis=-1)
    table = np.stack([real_rows, imag_rows], axis=2)
    return split_table(table.reshape(parts * GROUP * 2 * SHARE, 2 * DOPK))


def halves(value):
    high = value.astype(jnp.bfloat16)
    low = (value - high.astype(jnp.float32)).astype(jnp.bfloat16)
    return high, low


def product(value, high_table, low_table):
    rows = value.shape[0]
    high, low = halves(value)
    both = jnp.dot(
        jnp.concatenate([high, low], axis=0), high_table, preferred_element_type=jnp.float32
    )
    small = jnp.dot(high, low_table, preferred_element_type=jnp.float32)
    return both[:rows] + (both[rows:] + small)


def store_spectra(mixed, ref, slot):
    rows, half = mixed.shape[0] // 2, mixed.shape[1] // 2
    a_cos, a_sin = mixed[:rows, :half], mixed[:rows, half:]
    b_cos, b_sin = mixed[rows:, :half], mixed[rows:, half:]
    ref[slot, :, 0 * half : 1 * half] = a_cos + b_sin
    ref[slot, :, 1 * half : 2 * half] = b_cos - a_sin
    ref[slot, :, 2 * half : 3 * half] = a_cos - b_sin
    ref[slot, :, 3 * half : 4 * half] = b_cos + a_sin


def turned(value, steps):
    rows = value.shape[0]
    near = pltpu.roll(value, steps % rows, 0)
    far = pltpu.roll(value, (steps - BLOCKS if steps > 0 else steps + BLOCKS) % rows, 0)
    index = lax.broadcasted_iota(jnp.int32, value.shape, 0) % BLOCKS
    return jnp.where(index == (0 if steps > 0 else BLOCKS - 1), far, near)


def row_sums(values):
    index = lax.broadcasted_iota(jnp.int32, values[0].shape, 0)
    step = 1
    while len(values) > 1:
        first = index // step % 2 == 0
        values = [
            jnp.where(first, a, b) + pltpu.roll(jnp.where(first, b, a), step, 0)
            for a, b in zip(values[0::2], values[1::2])
        ]
        step *= 2
    return values[0]


def kernel(
    planes,
    parts,
    x_ref,
    fwd_hbm,
    inv_hbm,
    dop_hbm,
    out_ref,
    buf,
    qs,
    ps,
    srow,
    ct,
    rin,
    rlow,
    merged,
    fin,
    fwd,
    inv,
    dop,
    table_sem,
    send_plane,
    send_z,
    recv_x,
    send_c,
    recv_in,
    recv_low,
    send_t,
    recv_t,
):
    rx, tm = lax.axis_index("rx"), lax.axis_index("tm")
    count = planes * GROUP
    me = rx % GROUP
    base = rx - me
    share = SHARE * UNITS

    def other(k):
        return (me // 2 + k // 2) % 2 * 2 + (me % 2 + k % 2) % 2

    tables = [
        pltpu.make_async_copy(fwd_hbm, fwd, table_sem.at[0]),
        pltpu.make_async_copy(inv_hbm, inv, table_sem.at[1]),
        pltpu.make_async_copy(dop_hbm, dop, table_sem.at[2]),
    ]
    for copy in tables:
        copy.start()

    def part_of_x(index):
        return x_ref.at[:, pl.ds(pl.multiple_of(index * share, share), share), :]

    own = pltpu.make_async_copy(part_of_x(me), buf.at[me], recv_x.at[me])
    own.start()

    barrier = pltpu.get_barrier_semaphore()
    for k in range(1, GROUP):
        pl.semaphore_signal(barrier, 1, device_id=(base + other(k), tm), device_id_type=MESH)
    below = (base + count - GROUP) % count
    above = (base + GROUP) % count
    for j in range(GROUP):
        pl.semaphore_signal(barrier, 1, device_id=(below + j, tm), device_id_type=MESH)
    pl.semaphore_signal(barrier, 1, device_id=(above + me, tm), device_id_type=MESH)
    for k in range(1, parts):
        pl.semaphore_signal(barrier, 1, device_id=(rx, (tm + k) % parts), device_id_type=MESH)
    pl.semaphore_wait(barrier, GROUP - 1 + GROUP + 1 + parts - 1)

    def plane_copy(k):
        j = other(k)
        return pltpu.make_async_remote_copy(
            src_ref=part_of_x(j),
            dst_ref=buf.at[me],
            send_sem=send_plane.at[k - 1],
            recv_sem=recv_x.at[me],
            device_id=(base + j, tm),
            device_id_type=MESH,
        )

    def z_copy(k, src):
        j = other(k)
        return pltpu.make_async_remote_copy(
            src_ref=src,
            dst_ref=buf.at[GROUP + j],
            send_sem=send_z.at[k],
            recv_sem=recv_x.at[GROUP + j],
            device_id=((rx + count + (j // 2 * 2 - 1) * GROUP) % count, tm),
            device_id_type=MESH,
        )

    def arrival(slot):
        return pltpu.make_async_remote_copy(
            src_ref=buf.at[slot],
            dst_ref=buf.at[slot],
            send_sem=send_z.at[0],
            recv_sem=recv_x.at[slot],
            device_id=(rx, tm),
            device_id_type=MESH,
        )

    for k in (3, 2, 1):
        plane_copy(k).start()
    z_copy(0, part_of_x(me)).start()
    tables[0].wait()

    def pieces(slot, comp):
        rows = buf.at[slot, comp]
        even = rows[pl.ds(0, share // 2, stride=2), :]
        odd = rows[pl.ds(1, share // 2, stride=2), :]
        return even, odd

    def window_spectra(slot, target):
        rows = []
        for comp in range(2):
            even, odd = pieces(slot, comp)
            rows.append(jnp.concatenate([turned(odd, 1), even, odd, turned(even, -1)], axis=1))
        mixed = product(jnp.concatenate(rows, axis=0), fwd[0], fwd[1])
        store_spectra(mixed, qs, target)

    def block_spectra(slot, target):
        rows = [jnp.concatenate(pieces(slot, comp), axis=1) for comp in range(2)]
        mixed = product(
            jnp.concatenate(rows, axis=0), fwd[0, : WINDOW // 2], fwd[1, : WINDOW // 2]
        )
        store_spectra(mixed, ps, target)

    def plane_step(k, carry):
        j = other(k)

        @pl.when(k == 0)
        def _():
            own.wait()

        @pl.when(k > 0)
        def _():
            arrival(j).wait_recv()
            z_copy(k, buf.at[j]).start()

        window_spectra(j, j)
        block_spectra(j, j)
        return carry

    lax.fori_loop(0, GROUP, plane_step, 0)

    def z_step(k, carry):
        j = other(k)
        arrival(GROUP + j).wait_recv()

        @pl.when(j < 2)
        def _():
            window_spectra(GROUP + j, GROUP + j)

        @pl.when(j >= 2)
        def _():
            block_spectra(GROUP + j, GROUP + j - 2)

        return carry

    lax.fori_loop(0, GROUP, z_step, 0)

    def half_step(half, carry):
        def part(ref, slot, seg, index):
            start = pl.multiple_of(index * (WINDOW // 2) + half * LANES, LANES)
            return ref[slot, seg * BLOCKS : (seg + 1) * BLOCKS, pl.ds(start, LANES)]

        pair = 0
        for slot, partners in enumerate(PAIRS):
            for _, far in partners:
                sums = []
                for seg in range(SHARE):
                    q = [part(qs, slot, seg, i) for i in range(4)]
                    p = [part(ps, far, seg, i) for i in range(4)]
                    z = [
                        q[0] * p[0] + q[1] * p[1],
                        q[1] * p[0] - q[0] * p[1],
                        q[2] * p[2] + q[3] * p[3],
                        q[3] * p[2] - q[2] * p[3],
                    ]
                    z = [v[:8] + v[8:] for v in z]
                    sums.append([z[0] + z[2], z[3] - z[1], z[1] + z[3], z[0] - z[2]])
                for i in range(2):
                    rows = [v[i] for v in sums] + [v[2 + i] for v in sums]
                    start = pl.multiple_of(i * (WINDOW // 2) + half * LANES, LANES)
                    srow[pair * 8 : pair * 8 + 8, pl.ds(start, LANES)] = row_sums(rows)
                pair += 1
        return carry

    lax.fori_loop(0, 2, half_step, 0)

    tables[1].wait()
    corr = product(srow[...], inv[0], inv[1])
    lane = lax.broadcasted_iota(jnp.int32, (8, LANES), 1)
    pair = 0
    for slot, partners in enumerate(PAIRS):
        for part in range(parts):
            col, piece = part // 4, part % 4
            tile = jnp.zeros((8, LANES), jnp.float32)
            for index, (off, _) in enumerate(partners):
                row = (pair + index) * 8
                value = corr[row : row + 8, col * LANES : (col + 1) * LANES]
                shift = LAG_DEV * (off - piece) % LANES
                if shift:
                    value = pltpu.roll(value, shift, 1)
                tile = jnp.where(lane // LAG_DEV == off, value, tile)
            ct[slot, part] = tile
        pair += len(partners)

    def corr_copy(k):
        j = other(k)
        return pltpu.make_async_remote_copy(
            src_ref=ct.at[j],
            dst_ref=rin.at[me],
            send_sem=send_c.at[k - 1],
            recv_sem=recv_in.at[me],
            device_id=(base + j, tm),
            device_id_type=MESH,
        )

    def low_copy(i):
        return pltpu.make_async_remote_copy(
            src_ref=ct.at[GROUP + i],
            dst_ref=rlow.at[me],
            send_sem=send_c.at[GROUP - 1 + i],
            recv_sem=recv_low.at[me],
            device_id=(above + i, tm),
            device_id_type=MESH,
        )

    for i in range(2):
        low_copy(i).start()
    for k in (3, 2, 1):
        corr_copy(k).start()
    own_c = pltpu.make_async_copy(ct.at[me], rin.at[me], recv_in.at[me])
    own_c.start()
    own_c.wait()

    def corr_arrival(ref, sems, slot):
        return pltpu.make_async_remote_copy(
            src_ref=ref.at[slot],
            dst_ref=ref.at[slot],
            send_sem=send_c.at[0],
            recv_sem=sems.at[slot],
            device_id=(rx, tm),
            device_id_type=MESH,
        )

    for k in range(1, GROUP):
        corr_arrival(rin, recv_in, other(k)).wait_recv()

    @pl.when(me < 2)
    def _():
        for slot in range(GROUP):
            corr_arrival(rlow, recv_low, slot).wait_recv()

    kept = lane < 2 * LAG_DEV + LAG_DEV * me
    for part in range(parts):
        for slot in range(GROUP):
            merged[part, slot * 8 : slot * 8 + 8] = jnp.where(
                kept, rin[slot, part], rlow[slot, part]
            )

    def lag_copy(k):
        to = (tm + k) % parts
        return pltpu.make_async_remote_copy(
            src_ref=merged.at[to],
            dst_ref=fin.at[tm],
            send_sem=send_t.at[k - 1],
            recv_sem=recv_t.at[k - 1],
            device_id=(rx, to),
            device_id_type=MESH,
        )

    for k in range(1, parts):
        lag_copy(k).start()
    fin[tm] = merged[tm]
    tables[2].wait()
    for k in range(1, parts):
        source = (tm + parts - k) % parts
        pltpu.make_async_remote_copy(
            src_ref=fin.at[source],
            dst_ref=fin.at[source],
            send_sem=send_t.at[k - 1],
            recv_sem=recv_t.at[k - 1],
            device_id=(rx, tm),
            device_id_type=MESH,
        ).wait_recv()

    columns = fin[...].reshape(parts * GROUP * 2 * SHARE, LANES)
    result = product(columns.T, dop[0], dop[1])
    for off in range(OFFS):
        for col in range(4):
            out_ref[pl.ds(col // 2 * 8 + off * 2 + col % 2, LAG_DEV, stride=16), :] = result[
                off * LAG_DEV : (off + 1) * LAG_DEV, col * LANES : (col + 1) * LANES
            ]

    for k in range(1, GROUP):
        plane_copy(k).wait_send()
        corr_copy(k).wait_send()
    for k in range(GROUP):
        z_copy(k, buf.at[0]).wait_send()
    for i in range(2):
        low_copy(i).wait_send()
    for k in range(1, parts):
        lag_copy(k).wait_send()


def per_device(planes, parts, signals):
    rows = signals.reshape(2, -1, LANES)
    dop_rows = parts * GROUP * 2 * SHARE
    dma, vmem = pltpu.SemaphoreType.DMA, pltpu.VMEM
    out = pl.pallas_call(
        functools.partial(kernel, planes, parts),
        out_shape=jax.ShapeDtypeStruct((LAG_DEV * 2 * OFFS * 2, LANES), jnp.float32),
        in_specs=[pl.BlockSpec(memory_space=pl.ANY)] * 4,
        out_specs=pl.BlockSpec(memory_space=pltpu.VMEM),
        scratch_shapes=[
            vmem((2 * GROUP, 2, SHARE * UNITS, LANES), jnp.float32),
            vmem((6, SHARE * BLOCKS, 2 * WINDOW), jnp.float32),
            vmem((6, SHARE * BLOCKS, 2 * WINDOW), jnp.float32),
            vmem((16 * 8, WINDOW), jnp.float32),
            vmem((6, parts, 8, LANES), jnp.float32),
            vmem((GROUP, parts, 8, LANES), jnp.float32),
            vmem((GROUP, parts, 8, LANES), jnp.float32),
            vmem((parts, GROUP * 8, LANES), jnp.float32),
            vmem((parts, GROUP * 8, LANES), jnp.float32),
            vmem((2, WINDOW, WINDOW), jnp.bfloat16),
            vmem((2, WINDOW, LAGS), jnp.bfloat16),
            vmem((2, dop_rows, 2 * DOPK), jnp.bfloat16),
            dma((3,)),
            dma((GROUP - 1,)),
            dma((GROUP,)),
            dma((2 * GROUP,)),
            dma((GROUP + 1,)),
            dma((GROUP,)),
            dma((GROUP,)),
            dma((parts - 1,)),
            dma((parts - 1,)),
        ],
        compiler_params=pltpu.CompilerParams(
            collective_id=0, has_side_effects=True, vmem_limit_bytes=48 * 1024 * 1024
        ),
        name="ambiguity",
    )(
        rows,
        jnp.asarray(forward_table()),
        jnp.asarray(inverse_table()),
        jnp.asarray(doppler_table(parts)),
    )
    return out.reshape(LAG_DEV, 2, 1, OFFS, 1, DOPK)


def solution(mesh):
    planes, parts = mesh.shape["rx"] // GROUP, mesh.shape["tm"]
    return jax.shard_map(
        functools.partial(per_device, planes, parts),
        mesh=mesh,
        in_specs=(P(None, "rx", "tm"),),
        out_specs=P("tm", None, "rx", None, None, None),
        check_vma=False,
    )
```

time: 68.3 us -> 40.6 us (0.59)
  the two profiles are of different devices: /device:TPU:17 before, /device:TPU:96 now
where the time goes in v2:
time: 40.6 us; the launch traced here: 40.4 us
  Pallas kernels  35.3 us (87%)
  local copies, waits for them, and re-layouts  5.05 us (12%)
    pallas_call x1, Pallas kernels, per_device(): pl.pallas_call(functools.partial(kernel, planes, parts), out_shape=jax.Sh...  35.3 us
    unnamed x9, local copies, waits for them, and re-layouts  5.05 us

profile of v2, /device:TPU:96, one launch (start us, length us, event | category | flops | bytes accessed | tf_op | source)
XLA Modules:
  0.0 40.4 jit_solution(8380230939224721247)
XLA Ops:
  0.0 0.0 copy-start
  0.0 1.2 %copy-done = bf16[2,512,512]{2,1,0:T(8,128)(2,1)S(1)} copy-done((bf16[2,512,512]{2,1,0:T(8,128)(2,1)S(1)}, bf16[2,512,512]{2,1,0:T(8,128)(2,1)}, u32[]{:S(2)}) %copy-start) | copy-done | bytes 1048600
  1.2 0.0 copy-start.1
  1.2 1.0 %copy-done.1 = f32[2,1,65536]{2,1,0:T(1,128)S(1)} copy-done((f32[2,1,65536]{2,1,0:T(1,128)S(1)}, f32[2,1,65536]{2,1,0:T(1,128)}, u32[]{:S(2)}) %copy-start.1) | copy-done | bytes 524312
  2.3 0.0 copy-start.2
  2.3 1.0 %copy-done.2 = bf16[2,256,512]{2,1,0:T(8,128)(2,1)S(1)} copy-done((bf16[2,256,512]{2,1,0:T(8,128)(2,1)S(1)}, bf16[2,256,512]{2,1,0:T(8,128)(2,1)}, u32[]{:S(2)}) %copy-start.2) | copy-done | bytes 524312
  3.3 0.0 copy-start.3
  3.3 1.0 %copy-done.3 = bf16[2,512,256]{2,1,0:T(8,128)(2,1)S(1)} copy-done((bf16[2,512,256]{2,1,0:T(8,128)(2,1)S(1)}, bf16[2,512,256]{2,1,0:T(8,128)(2,1)}, u32[]{:S(2)}) %copy-start.3) | copy-done | bytes 524312
  4.4 35.3 %ambiguity.1 = f32[512,128]{1,0:T(8,128)S(1)} custom-call(f32[2,512,128]{2,1,0:T(8,128)S(1)} %bitcast.3, bf16[2,512,512]{2,1,0:T(8,128)(2,1)S(1)} %copy-done, bf16[2,512,256]{2,1,0:T(8,128)(2,1)S(1)} %copy-done.3, bf16[2,256,512]{2,1,0:T(8,128)(2,1)S(1)} %copy-done.2), custom_call_target="tpu_custom_call" | custom-call | tf_op jit(solution)/shard_map/ambiguity/pallas_call | solution.py:425
  39.7 0.7 %copy.7 = f32[32,2,1,4,1,256]{5,4,3,2,1,0:T(1,128)} copy(f32[32,2,1,4,1,256]{5,4,3,2,1,0:T(1,128)S(1)} %bitcast.2) | data formatting | bytes 524288
Async XLA Ops:
  0.0 1.2 %copy-start = (bf16[2,512,512]{2,1,0:T(8,128)(2,1)S(1)}, bf16[2,512,512]{2,1,0:T(8,128)(2,1)}, u32[]{:S(2)}) copy-start(bf16[2,512,512]{2,1,0:T(8,128)(2,1)} %constant.6.clone.fwd_hbm) | copy-start | bytes 3145732
  1.2 1.0 %copy-start.1 = (f32[2,1,65536]{2,1,0:T(1,128)S(1)}, f32[2,1,65536]{2,1,0:T(1,128)}, u32[]{:S(2)}) copy-start(f32[2,1,65536]{2,1,0:T(1,128)} %param.4) | copy-start | bytes 1572868
  2.3 1.0 %copy-start.2 = (bf16[2,256,512]{2,1,0:T(8,128)(2,1)S(1)}, bf16[2,256,512]{2,1,0:T(8,128)(2,1)}, u32[]{:S(2)}) copy-start(bf16[2,256,512]{2,1,0:T(8,128)(2,1)} %constant.8.clone.dop_hbm) | copy-start | bytes 1572868
  3.3 1.0 %copy-start.3 = (bf16[2,512,256]{2,1,0:T(8,128)(2,1)S(1)}, bf16[2,512,256]{2,1,0:T(8,128)(2,1)}, u32[]{:S(2)}) copy-start(bf16[2,512,256]{2,1,0:T(8,128)(2,1)} %constant.7.clone.inv_hbm) | copy-start | bytes 1572868

commit v3 on v1

v3 whole, which is shorter than its diff:
```python
import functools
import math

import jax
import jax.numpy as jnp
import ml_dtypes
import numpy as np
from jax import lax
from jax.experimental import pallas as pl
from jax.experimental.pallas import tpu as pltpu
from jax.sharding import PartitionSpec as P

SEG_LEN = 4096
LAGS = 256
DOPLEN = 512
DOPK = 256
OFFS = 4
WINDOW = 512
LANES = 128
GROUP = 4
SHARE = 4
UNITS = SEG_LEN // LANES
BLOCKS = SEG_LEN // 256
LAG_DEV = 32
VMEM_LIMIT = 67043328 - 384 * 1024

MESH = pl.DeviceIdType.MESH

PAIRS = (
    ((0, 5), (1, 4)),
    ((0, 0), (1, 5), (2, 4)),
    ((0, 1), (1, 0), (2, 5), (3, 4)),
    ((0, 2), (1, 1), (2, 0), (3, 5)),
    ((2, 1), (3, 0)),
    ((3, 1),),
)


def split_table(table):
    table = table.astype(np.float32)
    high = table.astype(ml_dtypes.bfloat16)
    low = (table - high.astype(np.float32)).astype(ml_dtypes.bfloat16)
    return np.stack([high, low])


def forward_table():
    sample = np.arange(WINDOW)[:, None]
    freq = np.arange(WINDOW // 2)[None, :] + 0.5
    angle = 2.0 * np.pi / WINDOW * sample * freq
    return split_table(np.concatenate([np.cos(angle), np.sin(angle)], axis=1))


def inverse_table():
    lag = np.arange(LAGS)[None, :]
    freq = np.arange(WINDOW // 2)[:, None] + 0.5
    angle = 2.0 * np.pi / WINDOW * lag * freq
    return split_table(np.concatenate([np.cos(angle), np.sin(angle)], axis=0) / WINDOW)


def doppler_table(parts):
    seg = np.arange(parts * GROUP * SHARE).reshape(parts, GROUP, SHARE, 1)
    freq = np.arange(DOPK) - DOPK // 2
    angle = 2.0 * np.pi / DOPLEN * (seg * freq % DOPLEN)
    scale = 1.0 / math.sqrt(2.0 * SEG_LEN * parts * GROUP * SHARE)
    cos, sin = np.cos(angle) * scale, -np.sin(angle) * scale
    real_rows = np.concatenate([cos, sin], axis=-1)
    imag_rows = np.concatenate([-sin, cos], axis=-1)
    table = np.stack([real_rows, imag_rows], axis=3)
    return split_table(table.reshape(parts * GROUP * 2 * SHARE, 2 * DOPK))


def halves(value):
    high = value.astype(jnp.bfloat16)
    low = (value - high.astype(jnp.float32)).astype(jnp.bfloat16)
    return high, low


def product(value, high_table, low_table):
    rows = value.shape[0]
    high, low = halves(value)
    both = jnp.dot(
        jnp.concatenate([high, low], axis=0), high_table, preferred_element_type=jnp.float32
    )
    small = jnp.dot(high, low_table, preferred_element_type=jnp.float32)
    return both[:rows] + (both[rows:] + small)


def store_spectra(mixed, ref, side, start):
    rows, half = mixed.shape[0] // 2, mixed.shape[1] // 2
    a_cos, a_sin = mixed[:rows, :half], mixed[:rows, half:]
    b_cos, b_sin = mixed[rows:, :half], mixed[rows:, half:]
    parts = (a_cos + b_sin, b_cos - a_sin, a_cos - b_sin, b_cos + a_sin)
    for index, part in enumerate(parts):
        ref[side, start : start + rows, index * half : (index + 1) * half] = part


def row_sums(values):
    index = lax.broadcasted_iota(jnp.int32, values[0].shape, 0)
    step = 1
    while len(values) > 1:
        first = index // step % 2 == 0
        values = [
            jnp.where(first, a, b) + pltpu.roll(jnp.where(first, b, a), step, 0)
            for a, b in zip(values[0::2], values[1::2])
        ]
        step *= 2
    return values[0]


def kernel(
    planes,
    parts,
    x_ref,
    fwd_hbm,
    inv_hbm,
    dop_hbm,
    out_ref,
    buf,
    qs,
    ps,
    srow,
    corr,
    ct,
    fin,
    low,
    fwd,
    inv,
    dop,
    table_sem,
    send_plane,
    send_z,
    recv_x,
    send_c,
    recv_c,
):
    rx, tm = lax.axis_index("rx"), lax.axis_index("tm")
    count = planes * GROUP
    me = rx % GROUP
    base = rx - me
    below = (base + count - GROUP) % count
    above = (base + GROUP) % count

    def other(k):
        return (me // 2 + k // 2) % 2 * 2 + (me % 2 + k % 2) % 2

    def part_of_x(index, seg):
        start = pl.multiple_of((index * SHARE + seg) * UNITS, UNITS)
        return x_ref.at[:, pl.ds(start, UNITS), :]

    def own_copy(seg):
        return pltpu.make_async_copy(part_of_x(me, seg), buf.at[me, seg], recv_x.at[me, seg])

    def plane_copy(k, seg):
        j = other(k)
        return pltpu.make_async_remote_copy(
            src_ref=part_of_x(j, seg),
            dst_ref=buf.at[me, seg],
            send_sem=send_plane.at[k - 1, seg],
            recv_sem=recv_x.at[me, seg],
            device_id=(base + j, tm),
            device_id_type=MESH,
        )

    def z_copy(k, seg, src):
        j = other(k)
        return pltpu.make_async_remote_copy(
            src_ref=src,
            dst_ref=buf.at[GROUP + j, seg],
            send_sem=send_z.at[k, seg],
            recv_sem=recv_x.at[GROUP + j, seg],
            device_id=((rx + count + (j // 2 * 2 - 1) * GROUP) % count, tm),
            device_id_type=MESH,
        )

    def received(ref, sem):
        return pltpu.make_async_remote_copy(
            src_ref=ref,
            dst_ref=ref,
            send_sem=send_c.at[0],
            recv_sem=sem,
            device_id=(rx, tm),
            device_id_type=MESH,
        )

    tables = [
        pltpu.make_async_copy(fwd_hbm, fwd, table_sem.at[0]),
        pltpu.make_async_copy(inv_hbm, inv, table_sem.at[1]),
        pltpu.make_async_copy(dop_hbm, dop, table_sem.at[2]),
    ]

    barrier = pltpu.get_barrier_semaphore()

    def greet(r, t):
        pl.semaphore_signal(barrier, 1, device_id=(r, t), device_id_type=MESH)

    greet(below + me, tm)
    greet(above + me, tm)
    for k in range(GROUP):
        for step in range(parts):
            if k or step:
                greet(base + other(k), (tm + step) % parts)

    @pl.when(me < 2)
    def _():
        for k in range(GROUP):
            for step in range(parts):
                greet(below + other(k), (tm + step) % parts)

    for copy in tables:
        copy.start()
    for seg in range(SHARE):
        own_copy(seg).start()
    pl.semaphore_wait(barrier, 2 + GROUP * parts - 1 + 2 * parts)

    for seg in range(SHARE):
        for k in (3, 2, 1):
            plane_copy(k, seg).start()
        z_copy(0, seg, part_of_x(me, seg)).start()
    tables[0].wait()

    def pieces(slot, seg, comp):
        rows = buf.at[slot, seg, comp]
        even = rows[pl.ds(0, BLOCKS, stride=2), :]
        odd = rows[pl.ds(1, BLOCKS, stride=2), :]
        return even, odd

    def window(slot, seg, comp):
        even, odd = pieces(slot, seg, comp)
        before = pltpu.roll(odd, 1, 0)
        after = pltpu.roll(even, BLOCKS - 1, 0)
        return jnp.concatenate([before, even, odd, after], axis=1)

    def window_spectra(slots, seg, side):
        rows = [window(slot, seg, comp) for comp in range(2) for slot in slots]
        mixed = product(jnp.concatenate(rows, axis=0), fwd[0], fwd[1])
        store_spectra(mixed, qs, side, slots[0] * BLOCKS)

    def block_spectra(slots, seg, side, target):
        rows = [
            jnp.concatenate(pieces(slot, seg, comp), axis=1) for comp in range(2) for slot in slots
        ]
        mixed = product(
            jnp.concatenate(rows, axis=0), fwd[0, : WINDOW // 2], fwd[1, : WINDOW // 2]
        )
        store_spectra(mixed, ps, side, target * BLOCKS)

    order = [(slot, off, far) for slot, partners in enumerate(PAIRS) for off, far in partners]

    def correlate(seg, side):
        def half_step(half, carry):
            def part(ref, slot, index):
                start = pl.multiple_of(index * (WINDOW // 2) + half * LANES, LANES)
                return ref[side, slot * BLOCKS : (slot + 1) * BLOCKS, pl.ds(start, LANES)]

            for group in range(2):
                sums = []
                for slot, _, far in order[group * 8 : group * 8 + 8]:
                    q = [part(qs, slot, i) for i in range(4)]
                    p = [part(ps, far, i) for i in range(4)]
                    z = [
                        q[0] * p[0] + q[1] * p[1],
                        q[1] * p[0] - q[0] * p[1],
                        q[2] * p[2] + q[3] * p[3],
                        q[3] * p[2] - q[2] * p[3],
                    ]
                    z = [v[:8] + v[8:] for v in z]
                    sums.append([z[0] + z[2], z[3] - z[1], z[1] + z[3], z[0] - z[2]])
                for i in range(4):
                    row = pl.multiple_of(seg * 32 + i // 2 * 16 + group * 8, 8)
                    lane = pl.multiple_of(i % 2 * (WINDOW // 2) + half * LANES, LANES)
                    srow[pl.ds(row, 8), pl.ds(lane, LANES)] = row_sums([v[i] for v in sums])
            return carry

        lax.fori_loop(0, 2, half_step, 0)

    def seg_step(step, carry):
        @pl.when(step < SHARE)
        def _():
            for k in range(1, GROUP):
                j = other(k)
                received(buf.at[j, step], recv_x.at[j, step]).wait_recv()
                z_copy(k, step, buf.at[j, step]).start()
            own_copy(step).wait()
            window_spectra(range(0, 4), step, step % 2)
            block_spectra(range(0, 3), step, step % 2, 0)

        @pl.when(step > 0)
        def _():
            seg = step - 1
            for slot in range(GROUP, 2 * GROUP):
                received(buf.at[slot, seg], recv_x.at[slot, seg]).wait_recv()
            window_spectra(range(4, 6), seg, seg % 2)
            block_spectra(range(6, 8), seg, seg % 2, 4)
            correlate(seg, seg % 2)

        return carry

    lax.fori_loop(0, SHARE + 1, seg_step, 0)

    tables[1].wait()
    lags = product(srow[...], inv[0], inv[1])
    corr[0], corr[1] = lags[:, :LANES], lags[:, LANES:]
    lane = lax.broadcasted_iota(jnp.int32, (8, LANES), 1)
    for slot in range(6):
        for col in range(2):
            values = [
                (off, corr[col, pl.ds(index, 8, stride=16), :])
                for index, (at, off, _) in enumerate(order)
                if at == slot
            ]
            for piece in range(4):
                tile = jnp.zeros((8, LANES), jnp.float32)
                for off, value in values:
                    shift = LAG_DEV * (off - piece) % LANES
                    if shift:
                        value = pltpu.roll(value, shift, 1)
                    tile = jnp.where(lane // LAG_DEV == off, value, tile)
                if col * 4 + piece < parts:
                    ct[slot, col * 4 + piece] = tile

    def tile_copy(k, step):
        j, to = other(k), (tm + step) % parts
        return pltpu.make_async_remote_copy(
            src_ref=ct.at[j, to],
            dst_ref=fin.at[tm, me],
            send_sem=send_c.at[min(k, 1)],
            recv_sem=recv_c.at[min(k, 1)],
            device_id=(base + j, to),
            device_id_type=MESH,
        )

    def low_copy(i, step):
        to = (tm + step) % parts
        return pltpu.make_async_remote_copy(
            src_ref=ct.at[GROUP + i, to],
            dst_ref=low.at[tm, me],
            send_sem=send_c.at[2],
            recv_sem=recv_c.at[2],
            device_id=(above + i, to),
            device_id_type=MESH,
        )

    for step in range(parts):
        for i in range(2):
            low_copy(i, step).start()
        for k in (3, 2, 1, 0):
            if k or step:
                tile_copy(k, step).start()
    fin[tm, me] = ct[me, tm]
    tables[2].wait()

    @pl.when(me < 2)
    def _():
        received(low, recv_c.at[2]).wait_recv()

    received(fin.at[:, : GROUP - 1], recv_c.at[1]).wait_recv()
    received(fin.at[: parts - 1, 0], recv_c.at[0]).wait_recv()

    rows = parts * GROUP * 2 * SHARE
    lanes = lax.broadcasted_iota(jnp.int32, (rows, LANES), 1)
    columns = jnp.where(
        lanes < 2 * LAG_DEV + LAG_DEV * me,
        fin[...].reshape(rows, LANES),
        low[...].reshape(rows, LANES),
    )
    result = product(columns.T, dop[0], dop[1])
    for off in range(OFFS):
        for col in range(4):
            out_ref[pl.ds(col // 2 * 8 + off * 2 + col % 2, LAG_DEV, stride=16), :] = result[
                off * LAG_DEV : (off + 1) * LAG_DEV, col * LANES : (col + 1) * LANES
            ]

    for seg in range(SHARE):
        for k in range(GROUP):
            if k:
                plane_copy(k, seg).wait_send()
            z_copy(k, seg, buf.at[0, seg]).wait_send()

    def sent(ref, sem):
        pltpu.make_async_remote_copy(
            src_ref=ref,
            dst_ref=ref,
            send_sem=sem,
            recv_sem=recv_c.at[0],
            device_id=(rx, tm),
            device_id_type=MESH,
        ).wait_send()

    sent(ct.at[0, : parts - 1], send_c.at[0])
    sent(ct.at[: GROUP - 1], send_c.at[1])
    sent(ct.at[GROUP : GROUP + 2], send_c.at[2])


def per_device(planes, parts, signals):
    rows = signals.reshape(2, -1, LANES)
    dop_rows = parts * GROUP * 2 * SHARE
    dma, vmem = pltpu.SemaphoreType.DMA, pltpu.VMEM
    out = pl.pallas_call(
        functools.partial(kernel, planes, parts),
        out_shape=jax.ShapeDtypeStruct((LAG_DEV * 2 * OFFS * 2, LANES), jnp.float32),
        in_specs=[pl.BlockSpec(memory_space=pl.ANY)] * 4,
        out_specs=pl.BlockSpec(memory_space=pltpu.VMEM),
        scratch_shapes=[
            vmem((2 * GROUP, SHARE, 2, UNITS, LANES), jnp.float32),
            vmem((2, 6 * BLOCKS, 2 * WINDOW), jnp.float32),
            vmem((2, 6 * BLOCKS, 2 * WINDOW), jnp.float32),
            vmem((SHARE * 32, WINDOW), jnp.float32),
            vmem((2, SHARE * 32, LANES), jnp.float32),
            vmem((6, parts, 8, LANES), jnp.float32),
            vmem((parts, GROUP, 8, LANES), jnp.float32),
            vmem((parts, GROUP, 8, LANES), jnp.float32),
            vmem((2, WINDOW, WINDOW), jnp.bfloat16),
            vmem((2, WINDOW, LAGS), jnp.bfloat16),
            vmem((2, dop_rows, 2 * DOPK), jnp.bfloat16),
            dma((3,)),
            dma((GROUP - 1, SHARE)),
            dma((GROUP, SHARE)),
            dma((2 * GROUP, SHARE)),
            dma((3,)),
            dma((3,)),
        ],
        compiler_params=pltpu.CompilerParams(
            collective_id=0, has_side_effects=True, vmem_limit_bytes=VMEM_LIMIT
        ),
        name="ambiguity",
    )(
        rows,
        jnp.asarray(forward_table()),
        jnp.asarray(inverse_table()),
        jnp.asarray(doppler_table(parts)),
    )
    return out.reshape(LAG_DEV, 2, 1, OFFS, 1, DOPK)


def solution(mesh):
    planes, parts = mesh.shape["rx"] // GROUP, mesh.shape["tm"]
    return jax.shard_map(
        functools.partial(per_device, planes, parts),
        mesh=mesh,
        in_specs=(P(None, "rx", "tm"),),
        out_specs=P("tm", None, "rx", None, None, None),
        check_vma=False,
    )
```

time: 68.3 us -> 35.3 us (0.52)
  the two profiles are of different devices: /device:TPU:17 before, /device:TPU:1 now
where the time goes in v3:
time: 35.3 us; the launch traced here: 35.2 us
  Pallas kernels  33.4 us (95%)
  local copies, waits for them, and re-layouts  1.83 us (5%)
    pallas_call x1, Pallas kernels, per_device(): pl.pallas_call(functools.partial(kernel, planes, parts), out_shape=jax.Sh...  33.4 us
    unnamed x1, local copies, waits for them, and re-layouts  1.83 us

profile of v3, /device:TPU:1, one launch (start us, length us, event | category | flops | bytes accessed | tf_op | source)
XLA Modules:
  0.0 35.2 jit_solution(17691517299942350665)
XLA Ops:
  0.0 33.4 %ambiguity.1 = f32[512,128]{1,0:T(8,128)} custom-call(f32[2,512,128]{2,1,0:T(8,128)} %bitcast.3, bf16[2,512,512]{2,1,0:T(8,128)(2,1)} %constant.6.clone.fwd_hbm, bf16[2,512,256]{2,1,0:T(8,128)(2,1)} %constant.7.clone.inv_hbm, bf16[2,256,512]{2,1,0:T(8,128)(2,1)} %constant.8.clone.dop_hbm), custom_call_target="tpu_custom_call" | custom-call | tf_op jit(solution)/shard_map/ambiguity/pallas_call | solution.py:398
  33.4 1.8 %copy.7 = f32[32,2,1,4,1,256]{5,4,3,2,1,0:T(1,128)} copy(f32[32,2,1,4,1,256]{5,4,3,2,1,0:T(1,128)} %bitcast.2) | data formatting | bytes 524288

commit v4 on v3

--- a/solution.py
+++ b/solution.py
@@ -22,7 +22,7 @@
 UNITS = SEG_LEN // LANES
 BLOCKS = SEG_LEN // 256
 LAG_DEV = 32
-VMEM_LIMIT = 67043328 - 384 * 1024
+VMEM_LIMIT = 67043328 - 500 * 1024
 
 MESH = pl.DeviceIdType.MESH
 
@@ -61,8 +61,7 @@
     seg = np.arange(parts * GROUP * SHARE).reshape(parts, GROUP, SHARE, 1)
     freq = np.arange(DOPK) - DOPK // 2
     angle = 2.0 * np.pi / DOPLEN * (seg * freq % DOPLEN)
-    scale = 1.0 / math.sqrt(2.0 * SEG_LEN * parts * GROUP * SHARE)
-    cos, sin = np.cos(angle) * scale, -np.sin(angle) * scale
+    cos, sin = np.cos(angle), -np.sin(angle)
     real_rows = np.concatenate([cos, sin], axis=-1)
     imag_rows = np.concatenate([-sin, cos], axis=-1)
     table = np.stack([real_rows, imag_rows], axis=3)
@@ -273,29 +272,26 @@
 
         lax.fori_loop(0, 2, half_step, 0)
 
-    def seg_step(step, carry):
-        @pl.when(step < SHARE)
-        def _():
-            for k in range(1, GROUP):
-                j = other(k)
-                received(buf.at[j, step], recv_x.at[j, step]).wait_recv()
-                z_copy(k, step, buf.at[j, step]).start()
-            own_copy(step).wait()
-            window_spectra(range(0, 4), step, step % 2)
-            block_spectra(range(0, 3), step, step % 2, 0)
-
-        @pl.when(step > 0)
-        def _():
-            seg = step - 1
-            for slot in range(GROUP, 2 * GROUP):
-                received(buf.at[slot, seg], recv_x.at[slot, seg]).wait_recv()
-            window_spectra(range(4, 6), seg, seg % 2)
-            block_spectra(range(6, 8), seg, seg % 2, 4)
-            correlate(seg, seg % 2)
-
+    def plane_step(seg, carry):
+        for k in range(1, GROUP):
+            j = other(k)
+            received(buf.at[j, seg], recv_x.at[j, seg]).wait_recv()
+            z_copy(k, seg, buf.at[j, seg]).start()
+        own_copy(seg).wait()
+        window_spectra(range(0, 4), seg, seg)
+        block_spectra(range(0, 3), seg, seg, 0)
         return carry
 
-    lax.fori_loop(0, SHARE + 1, seg_step, 0)
+    def z_step(seg, carry):
+        for slot in range(GROUP, 2 * GROUP):
+            received(buf.at[slot, seg], recv_x.at[slot, seg]).wait_recv()
+        window_spectra(range(4, 6), seg, seg)
+        block_spectra(range(6, 8), seg, seg, 4)
+        correlate(seg, seg)
+        return carry
+
+    lax.fori_loop(0, SHARE, plane_step, 0)
+    lax.fori_loop(0, SHARE, z_step, 0)
 
     tables[1].wait()
     lags = product(srow[...], inv[0], inv[1])
@@ -402,8 +398,8 @@
         out_specs=pl.BlockSpec(memory_space=pltpu.VMEM),
         scratch_shapes=[
             vmem((2 * GROUP, SHARE, 2, UNITS, LANES), jnp.float32),
-            vmem((2, 6 * BLOCKS, 2 * WINDOW), jnp.float32),
-            vmem((2, 6 * BLOCKS, 2 * WINDOW), jnp.float32),
+            vmem((SHARE, 6 * BLOCKS, 2 * WINDOW), jnp.float32),
+            vmem((SHARE, 6 * BLOCKS, 2 * WINDOW), jnp.float32),
             vmem((SHARE * 32, WINDOW), jnp.float32),
             vmem((2, SHARE * 32, LANES), jnp.float32),
             vmem((6, parts, 8, LANES), jnp.float32),
@@ -429,7 +425,8 @@
         jnp.asarray(inverse_table()),
         jnp.asarray(doppler_table(parts)),
     )
-    return out.reshape(LAG_DEV, 2, 1, OFFS, 1, DOPK)
+    scale = 1.0 / math.sqrt(2.0 * SEG_LEN * parts * GROUP * SHARE)
+    return out.reshape(LAG_DEV, 2, 1, OFFS, 1, DOPK) * jnp.float32(scale)
 
 
 def solution(mesh):

time: 35.3 us -> 32.5 us (0.921)
  Pallas kernels: 33.4 us -> 30.7 us
  local copies, waits for them, and re-layouts: 1.83 us -> 0 us
  other arithmetic: 0 us -> 1.67 us
    pallas_call x1, Pallas kernels: 33.4 us -> 30.7 us  [per_device(): pl.pallas_call(functools.partial(kernel, planes, parts), out_shape=jax.Sh...]
    unnamed x1 -> x0, local copies, waits for them, and re-layouts: 1.83 us -> none
    mul x0 -> x1, other arithmetic: none -> 1.67 us  [per_device(): return out.reshape(LAG_DEV, 2, 1, OFFS, 1, DOPK) * jnp.float32(scale)]
where the time goes in v4:
time: 32.5 us; the launch traced here: 32.4 us
  Pallas kernels  30.7 us (94%)
  other arithmetic  1.67 us (5%)
    pallas_call x1, Pallas kernels, per_device(): pl.pallas_call(functools.partial(kernel, planes, parts), out_shape=jax.Sh...  30.7 us
    mul x1, other arithmetic, per_device(): return out.reshape(LAG_DEV, 2, 1, OFFS, 1, DOPK) * jnp.float32(scale)  1.67 us

profile of v4, /device:TPU:1, one launch (start us, length us, event | category | flops | bytes accessed | tf_op | source)
XLA Modules:
  0.0 32.4 jit_solution(3446497793180764458)
XLA Ops:
  0.0 30.7 %ambiguity.1 = f32[512,128]{1,0:T(8,128)} custom-call(f32[2,512,128]{2,1,0:T(8,128)} %bitcast.2, bf16[2,512,512]{2,1,0:T(8,128)(2,1)} %constant.8.clone.fwd_hbm, bf16[2,512,256]{2,1,0:T(8,128)(2,1)} %constant.9.clone.inv_hbm, bf16[2,256,512]{2,1,0:T(8,128)(2,1)} %constant.10.clone.dop_hbm), custom_call_target="tpu_custom_call" | custom-call | tf_op jit(solution)/shard_map/ambiguity/pallas_call | solution.py:394
  30.7 1.7 %broadcast_multiply_fusion = f32[512,128]{1,0:T(8,128)} fusion(f32[512,128]{1,0:T(8,128)} %ambiguity.1), kind=kLoop, calls=%fused_computation | loop fusion | flops 65536 | bytes 524288 | tf_op jit(solution)/shard_map/mul | solution.py:429

commit v5 on v4

--- a/solution.py
+++ b/solution.py
@@ -22,7 +22,11 @@
 UNITS = SEG_LEN // LANES
 BLOCKS = SEG_LEN // 256
 LAG_DEV = 32
-VMEM_LIMIT = 67043328 - 500 * 1024
+SPLIT = 2
+CHUNKS = SHARE * SPLIT
+LAG_STEPS = 2
+CHUNK = UNITS // SPLIT
+VMEM_LIMIT = 67043328 - 10800 * 1024
 
 MESH = pl.DeviceIdType.MESH
 
@@ -131,6 +135,7 @@
     recv_x,
     send_c,
     recv_c,
+    ready,
 ):
     rx, tm = lax.axis_index("rx"), lax.axis_index("tm")
     count = planes * GROUP
@@ -142,31 +147,38 @@
     def other(k):
         return (me // 2 + k // 2) % 2 * 2 + (me % 2 + k % 2) % 2
 
-    def part_of_x(index, seg):
-        start = pl.multiple_of((index * SHARE + seg) * UNITS, UNITS)
-        return x_ref.at[:, pl.ds(start, UNITS), :]
+    def part_of_x(index, chunk):
+        start = pl.multiple_of((index * CHUNKS + chunk) * CHUNK, CHUNK)
+        return x_ref.at[:, pl.ds(start, CHUNK), :]
+
+    def place(slot, chunk):
+        start = pl.multiple_of(chunk % SPLIT * CHUNK, CHUNK)
+        return buf.at[slot, chunk // SPLIT, :, pl.ds(start, CHUNK), :]
 
     def own_copy(seg):
-        return pltpu.make_async_copy(part_of_x(me, seg), buf.at[me, seg], recv_x.at[me, seg])
-
-    def plane_copy(k, seg):
+        start = pl.multiple_of((me * SHARE + seg) * UNITS, UNITS)
+        return pltpu.make_async_copy(
+            x_ref.at[:, pl.ds(start, UNITS), :], buf.at[me, seg], recv_x.at[me, seg]
+        )
+
+    def plane_copy(k, chunk):
         j = other(k)
         return pltpu.make_async_remote_copy(
-            src_ref=part_of_x(j, seg),
-            dst_ref=buf.at[me, seg],
-            send_sem=send_plane.at[k - 1, seg],
-            recv_sem=recv_x.at[me, seg],
+            src_ref=part_of_x(j, chunk),
+            dst_ref=place(me, chunk),
+            send_sem=send_plane.at[k - 1, chunk],
+            recv_sem=recv_x.at[me, chunk],
             device_id=(base + j, tm),
             device_id_type=MESH,
         )
 
-    def z_copy(k, seg, src):
+    def z_copy(k, chunk, src):
         j = other(k)
         return pltpu.make_async_remote_copy(
             src_ref=src,
-            dst_ref=buf.at[GROUP + j, seg],
-            send_sem=send_z.at[k, seg],
-            recv_sem=recv_x.at[GROUP + j, seg],
+            dst_ref=place(GROUP + j, chunk),
+            send_sem=send_z.at[k, chunk],
+            recv_sem=recv_x.at[GROUP + j, chunk],
             device_id=((rx + count + (j // 2 * 2 - 1) * GROUP) % count, tm),
             device_id_type=MESH,
         )
@@ -194,28 +206,32 @@
 
     greet(below + me, tm)
     greet(above + me, tm)
-    for k in range(GROUP):
-        for step in range(parts):
-            if k or step:
-                greet(base + other(k), (tm + step) % parts)
-
-    @pl.when(me < 2)
-    def _():
-        for k in range(GROUP):
-            for step in range(parts):
-                greet(below + other(k), (tm + step) % parts)
-
+    for k in range(1, GROUP):
+        greet(base + other(k), tm)
+    for step in range(1, parts):
+        greet(rx, (tm + step) % parts)
     for copy in tables:
         copy.start()
     for seg in range(SHARE):
         own_copy(seg).start()
-    pl.semaphore_wait(barrier, 2 + GROUP * parts - 1 + 2 * parts)
-
-    for seg in range(SHARE):
+    pl.semaphore_wait(barrier, 2 + GROUP - 1 + parts - 1)
+
+    for chunk in range(CHUNKS):
         for k in (3, 2, 1):
-            plane_copy(k, seg).start()
-        z_copy(0, seg, part_of_x(me, seg)).start()
+            plane_copy(k, chunk).start()
+        z_copy(0, chunk, part_of_x(me, chunk)).start()
+
+    for k in range(1, GROUP):
+        pl.semaphore_signal(ready.at[0], 1, device_id=(base + other(k), tm), device_id_type=MESH)
+    pl.semaphore_signal(ready.at[1], 1, device_id=(above + me, tm), device_id_type=MESH)
     tables[0].wait()
+    pl.semaphore_wait(ready.at[1], 1)
+
+    @pl.when(me < 2)
+    def _():
+        for k in range(GROUP):
+            to = below + other(k)
+            pl.semaphore_signal(ready.at[2], 1, device_id=(to, tm), device_id_type=MESH)
 
     def pieces(slot, seg, comp):
         rows = buf.at[slot, seg, comp]
@@ -272,26 +288,34 @@
 
         lax.fori_loop(0, 2, half_step, 0)
 
-    def plane_step(seg, carry):
-        for k in range(1, GROUP):
-            j = other(k)
-            received(buf.at[j, seg], recv_x.at[j, seg]).wait_recv()
-            z_copy(k, seg, buf.at[j, seg]).start()
-        own_copy(seg).wait()
-        window_spectra(range(0, 4), seg, seg)
-        block_spectra(range(0, 3), seg, seg, 0)
+    def arrived(slot, chunk):
+        received(place(slot, chunk), recv_x.at[slot, chunk]).wait_recv()
+
+    def seg_step(step, carry):
+        @pl.when(step < SHARE)
+        def _():
+            for part in range(SPLIT):
+                chunk = step * SPLIT + part
+                for k in range(1, GROUP):
+                    arrived(other(k), chunk)
+                    z_copy(k, chunk, place(other(k), chunk)).start()
+            own_copy(step).wait()
+            window_spectra(range(0, 4), step, step)
+            block_spectra(range(0, 3), step, step, 0)
+
+        @pl.when(step >= LAG_STEPS)
+        def _():
+            seg = step - LAG_STEPS
+            for part in range(SPLIT):
+                for slot in range(GROUP, 2 * GROUP):
+                    arrived(slot, seg * SPLIT + part)
+            window_spectra(range(4, 6), seg, seg)
+            block_spectra(range(6, 8), seg, seg, 4)
+            correlate(seg, seg)
+
         return carry
 
-    def z_step(seg, carry):
-        for slot in range(GROUP, 2 * GROUP):
-            received(buf.at[slot, seg], recv_x.at[slot, seg]).wait_recv()
-        window_spectra(range(4, 6), seg, seg)
-        block_spectra(range(6, 8), seg, seg, 4)
-        correlate(seg, seg)
-        return carry
-
-    lax.fori_loop(0, SHARE, plane_step, 0)
-    lax.fori_loop(0, SHARE, z_step, 0)
+    lax.fori_loop(0, SHARE + LAG_STEPS, seg_step, 0)
 
     tables[1].wait()
     lags = product(srow[...], inv[0], inv[1])
@@ -336,6 +360,8 @@
             device_id_type=MESH,
         )
 
+    pl.semaphore_wait(ready.at[0], GROUP - 1)
+    pl.semaphore_wait(ready.at[2], 2)
     for step in range(parts):
         for i in range(2):
             low_copy(i, step).start()
@@ -366,11 +392,11 @@
                 off * LAG_DEV : (off + 1) * LAG_DEV, col * LANES : (col + 1) * LANES
             ]
 
-    for seg in range(SHARE):
+    for chunk in range(CHUNKS):
         for k in range(GROUP):
             if k:
-                plane_copy(k, seg).wait_send()
-            z_copy(k, seg, buf.at[0, seg]).wait_send()
+                plane_copy(k, chunk).wait_send()
+            z_copy(k, chunk, part_of_x(me, chunk)).wait_send()
 
     def sent(ref, sem):
         pltpu.make_async_remote_copy(
@@ -409,11 +435,12 @@
             vmem((2, WINDOW, LAGS), jnp.bfloat16),
             vmem((2, dop_rows, 2 * DOPK), jnp.bfloat16),
             dma((3,)),
-            dma((GROUP - 1, SHARE)),
-            dma((GROUP, SHARE)),
-            dma((2 * GROUP, SHARE)),
+            dma((GROUP - 1, CHUNKS)),
+            dma((GROUP, CHUNKS)),
+            dma((2 * GROUP, CHUNKS)),
             dma((3,)),
             dma((3,)),
+            pltpu.SemaphoreType.REGULAR((3,)),
         ],
         compiler_params=pltpu.CompilerParams(
             collective_id=0, has_side_effects=True, vmem_limit_bytes=VMEM_LIMIT

time: 32.5 us -> 31.7 us (0.975)
  other arithmetic: 1.67 us -> 0.72 us
    mul x1, other arithmetic: 1.67 us -> 0.72 us  [per_device(): return out.reshape(LAG_DEV, 2, 1, OFFS, 1, DOPK) * jnp.float32(scale)]
where the time goes in v5:
time: 31.7 us
  Pallas kernels  30.9 us (97%)
  other arithmetic  0.72 us (2%)
    pallas_call x1, Pallas kernels, per_device(): pl.pallas_call(functools.partial(kernel, planes, parts), out_shape=jax.Sh...  30.9 us
    mul x1, other arithmetic, per_device(): return out.reshape(LAG_DEV, 2, 1, OFFS, 1, DOPK) * jnp.float32(scale)  0.72 us

profile of v5, /device:TPU:1, one launch (start us, length us, event | category | flops | bytes accessed | tf_op | source)
XLA Modules:
  0.0 31.7 jit_solution(13616594455660975022)
XLA Ops:
  0.0 30.9 %ambiguity.1 = f32[512,128]{1,0:T(8,128)S(1)} custom-call(f32[2,512,128]{2,1,0:T(8,128)} %bitcast.2, bf16[2,512,512]{2,1,0:T(8,128)(2,1)} %constant.8.clone.fwd_hbm, bf16[2,512,256]{2,1,0:T(8,128)(2,1)} %constant.9.clone.inv_hbm, bf16[2,256,512]{2,1,0:T(8,128)(2,1)} %constant.10.clone.dop_hbm), custom_call_target="tpu_custom_call" | custom-call | tf_op jit(solution)/shard_map/ambiguity/pallas_call | solution.py:420
  30.9 0.7 %broadcast_multiply_fusion = f32[512,128]{1,0:T(8,128)} fusion(f32[512,128]{1,0:T(8,128)S(1)} %ambiguity.1), kind=kLoop, calls=%fused_computation | loop fusion | flops 65536 | bytes 524288 | tf_op jit(solution)/shard_map/mul | solution.py:456

commit v6 on v5

--- a/solution.py
+++ b/solution.py
@@ -22,6 +22,7 @@
 UNITS = SEG_LEN // LANES
 BLOCKS = SEG_LEN // 256
 LAG_DEV = 32
+HALF_ROWS = SHARE
 SPLIT = 2
 CHUNKS = SHARE * SPLIT
 LAG_STEPS = 2
@@ -187,7 +188,7 @@
         return pltpu.make_async_remote_copy(
             src_ref=ref,
             dst_ref=ref,
-            send_sem=send_c.at[0],
+            send_sem=send_c.at[0, 0],
             recv_sem=sem,
             device_id=(rx, tm),
             device_id_type=MESH,
@@ -315,68 +316,95 @@
 
         return carry
 
-    lax.fori_loop(0, SHARE + LAG_STEPS, seg_step, 0)
-
+    lane = lax.broadcasted_iota(jnp.int32, (HALF_ROWS, LANES), 1)
+
+    def tile_copy(k, step, half):
+        j, to = other(k), (tm + step) % parts
+        rows = pl.ds(half * HALF_ROWS, HALF_ROWS)
+        return pltpu.make_async_remote_copy(
+            src_ref=ct.at[j, to, rows],
+            dst_ref=fin.at[tm, me, rows],
+            send_sem=send_c.at[half, min(k, 1)],
+            recv_sem=recv_c.at[half, min(k, 1)],
+            device_id=(base + j, to),
+            device_id_type=MESH,
+        )
+
+    def low_copy(i, step, half):
+        to = (tm + step) % parts
+        rows = pl.ds(half * HALF_ROWS, HALF_ROWS)
+        return pltpu.make_async_remote_copy(
+            src_ref=ct.at[GROUP + i, to, rows],
+            dst_ref=low.at[tm, me, rows],
+            send_sem=send_c.at[half, 2],
+            recv_sem=recv_c.at[half, 2],
+            device_id=(above + i, to),
+            device_id_type=MESH,
+        )
+
+    def tiles(slots, half):
+        first = half * SHARE * 16
+        for slot in slots:
+            for col in range(2):
+                values = [
+                    (off, corr[col, pl.ds(first + index, HALF_ROWS, stride=16), :])
+                    for index, (at, off, _) in enumerate(order)
+                    if at == slot
+                ]
+                for piece in range(4):
+                    if col * 4 + piece >= parts:
+                        continue
+                    tile = jnp.zeros((HALF_ROWS, LANES), jnp.float32)
+                    for off, value in values:
+                        shift = LAG_DEV * (off - piece) % LANES
+                        if shift:
+                            value = pltpu.roll(value, shift, 1)
+                        tile = jnp.where(lane // LAG_DEV == off, value, tile)
+                    rows = slice(half * HALF_ROWS, (half + 1) * HALF_ROWS)
+                    ct[slot, col * 4 + piece, rows] = tile
+
+    steps = sorted(range(parts), key=lambda step: -min(step % 4, -step % 4))
+
+    def send_lags(half):
+        rows = slice(half * SHARE * 16, (half + 1) * SHARE * 16)
+        lags = product(srow[rows], inv[0], inv[1])
+        corr[0, rows], corr[1, rows] = lags[:, :LANES], lags[:, LANES:]
+        tiles((4, 5), half)
+        for step in steps:
+            for i in range(2):
+                low_copy(i, step, half).start()
+        tiles(range(4), half)
+        for ks in ((3, 2), (1, 0)):
+            for step in steps:
+                for k in ks:
+                    if k or step:
+                        tile_copy(k, step, half).start()
+
+    lax.fori_loop(0, SHARE // 2 + LAG_STEPS, seg_step, 0)
     tables[1].wait()
-    lags = product(srow[...], inv[0], inv[1])
-    corr[0], corr[1] = lags[:, :LANES], lags[:, LANES:]
-    lane = lax.broadcasted_iota(jnp.int32, (8, LANES), 1)
-    for slot in range(6):
-        for col in range(2):
-            values = [
-                (off, corr[col, pl.ds(index, 8, stride=16), :])
-                for index, (at, off, _) in enumerate(order)
-                if at == slot
-            ]
-            for piece in range(4):
-                tile = jnp.zeros((8, LANES), jnp.float32)
-                for off, value in values:
-                    shift = LAG_DEV * (off - piece) % LANES
-                    if shift:
-                        value = pltpu.roll(value, shift, 1)
-                    tile = jnp.where(lane // LAG_DEV == off, value, tile)
-                if col * 4 + piece < parts:
-                    ct[slot, col * 4 + piece] = tile
-
-    def tile_copy(k, step):
-        j, to = other(k), (tm + step) % parts
-        return pltpu.make_async_remote_copy(
-            src_ref=ct.at[j, to],
-            dst_ref=fin.at[tm, me],
-            send_sem=send_c.at[min(k, 1)],
-            recv_sem=recv_c.at[min(k, 1)],
-            device_id=(base + j, to),
-            device_id_type=MESH,
-        )
-
-    def low_copy(i, step):
-        to = (tm + step) % parts
-        return pltpu.make_async_remote_copy(
-            src_ref=ct.at[GROUP + i, to],
-            dst_ref=low.at[tm, me],
-            send_sem=send_c.at[2],
-            recv_sem=recv_c.at[2],
-            device_id=(above + i, to),
-            device_id_type=MESH,
-        )
-
     pl.semaphore_wait(ready.at[0], GROUP - 1)
     pl.semaphore_wait(ready.at[2], 2)
-    for step in range(parts):
-        for i in range(2):
-            low_copy(i, step).start()
-        for k in (3, 2, 1, 0):
-            if k or step:
-                tile_copy(k, step).start()
+    send_lags(0)
+    lax.fori_loop(SHARE // 2 + LAG_STEPS, SHARE + LAG_STEPS, seg_step, 0)
+    send_lags(1)
+
     fin[tm, me] = ct[me, tm]
     tables[2].wait()
-
-    @pl.when(me < 2)
-    def _():
-        received(low, recv_c.at[2]).wait_recv()
-
-    received(fin.at[:, : GROUP - 1], recv_c.at[1]).wait_recv()
-    received(fin.at[: parts - 1, 0], recv_c.at[0]).wait_recv()
+    for chunk in range(CHUNKS):
+        for k in range(GROUP):
+            if k:
+                plane_copy(k, chunk).wait_send()
+            z_copy(k, chunk, part_of_x(me, chunk)).wait_send()
+
+    for half in range(2):
+        rows = pl.ds(half * HALF_ROWS, HALF_ROWS)
+
+        @pl.when(me < 2)
+        def _():
+            received(low.at[:, :, rows], recv_c.at[half, 2]).wait_recv()
+
+        received(fin.at[:, : GROUP - 1, rows], recv_c.at[half, 1]).wait_recv()
+        received(fin.at[: parts - 1, 0, rows], recv_c.at[half, 0]).wait_recv()
 
     rows = parts * GROUP * 2 * SHARE
     lanes = lax.broadcasted_iota(jnp.int32, (rows, LANES), 1)
@@ -392,25 +420,21 @@
                 off * LAG_DEV : (off + 1) * LAG_DEV, col * LANES : (col + 1) * LANES
             ]
 
-    for chunk in range(CHUNKS):
-        for k in range(GROUP):
-            if k:
-                plane_copy(k, chunk).wait_send()
-            z_copy(k, chunk, part_of_x(me, chunk)).wait_send()
-
     def sent(ref, sem):
         pltpu.make_async_remote_copy(
             src_ref=ref,
             dst_ref=ref,
             send_sem=sem,
-            recv_sem=recv_c.at[0],
+            recv_sem=recv_c.at[0, 0],
             device_id=(rx, tm),
             device_id_type=MESH,
         ).wait_send()
 
-    sent(ct.at[0, : parts - 1], send_c.at[0])
-    sent(ct.at[: GROUP - 1], send_c.at[1])
-    sent(ct.at[GROUP : GROUP + 2], send_c.at[2])
+    for half in range(2):
+        rows = pl.ds(half * HALF_ROWS, HALF_ROWS)
+        sent(ct.at[0, : parts - 1, rows], send_c.at[half, 0])
+        sent(ct.at[: GROUP - 1, :, rows], send_c.at[half, 1])
+        sent(ct.at[GROUP : GROUP + 2, :, rows], send_c.at[half, 2])
 
 
 def per_device(planes, parts, signals):
@@ -438,8 +462,8 @@
             dma((GROUP - 1, CHUNKS)),
             dma((GROUP, CHUNKS)),
             dma((2 * GROUP, CHUNKS)),
-            dma((3,)),
-            dma((3,)),
+            dma((2, 3)),
+            dma((2, 3)),
             pltpu.SemaphoreType.REGULAR((3,)),
         ],
         compiler_params=pltpu.CompilerParams(

time: 31.7 us -> 31 us (0.978)
  Pallas kernels: 30.9 us -> 30.2 us
    pallas_call x1, Pallas kernels: 30.9 us -> 30.2 us  [per_device(): pl.pallas_call(functools.partial(kernel, planes, parts), out_shape=jax.Sh...]
where the time goes in v6:
time: 31 us; the launch traced here: 30.9 us
  Pallas kernels  30.2 us (97%)
  other arithmetic  0.72 us (2%)
    pallas_call x1, Pallas kernels, per_device(): pl.pallas_call(functools.partial(kernel, planes, parts), out_shape=jax.Sh...  30.2 us
    mul x1, other arithmetic, per_device(): return out.reshape(LAG_DEV, 2, 1, OFFS, 1, DOPK) * jnp.float32(scale)  0.72 us

profile of v6, /device:TPU:1, one launch (start us, length us, event | category | flops | bytes accessed | tf_op | source)
XLA Modules:
  0.0 30.9 jit_solution(17996490374491550178)
XLA Ops:
  0.0 30.2 %ambiguity.1 = f32[512,128]{1,0:T(8,128)S(1)} custom-call(f32[2,512,128]{2,1,0:T(8,128)} %bitcast.2, bf16[2,512,512]{2,1,0:T(8,128)(2,1)} %constant.8.clone.fwd_hbm, bf16[2,512,256]{2,1,0:T(8,128)(2,1)} %constant.9.clone.inv_hbm, bf16[2,256,512]{2,1,0:T(8,128)(2,1)} %constant.10.clone.dop_hbm), custom_call_target="tpu_custom_call" | custom-call | tf_op jit(solution)/shard_map/ambiguity/pallas_call | solution.py:444
  30.2 0.7 %broadcast_multiply_fusion = f32[512,128]{1,0:T(8,128)} fusion(f32[512,128]{1,0:T(8,128)S(1)} %ambiguity.1), kind=kLoop, calls=%fused_computation | loop fusion | flops 65536 | bytes 524288 | tf_op jit(solution)/shard_map/mul | solution.py:480

commit v7 on v6

--- a/solution.py
+++ b/solution.py
@@ -23,9 +23,9 @@
 BLOCKS = SEG_LEN // 256
 LAG_DEV = 32
 HALF_ROWS = SHARE
-SPLIT = 2
+SPLIT = 1
 CHUNKS = SHARE * SPLIT
-LAG_STEPS = 2
+LAG_STEPS = 3
 CHUNK = UNITS // SPLIT
 VMEM_LIMIT = 67043328 - 10800 * 1024
 
@@ -131,9 +131,10 @@
     inv,
     dop,
     table_sem,
-    send_plane,
-    send_z,
-    recv_x,
+    own_sem,
+    send_x,
+    recv_plane,
+    recv_z,
     send_c,
     recv_c,
     ready,
@@ -153,22 +154,21 @@
         return x_ref.at[:, pl.ds(start, CHUNK), :]
 
     def place(slot, chunk):
-        start = pl.multiple_of(chunk % SPLIT * CHUNK, CHUNK)
-        return buf.at[slot, chunk // SPLIT, :, pl.ds(start, CHUNK), :]
-
-    def own_copy(seg):
-        start = pl.multiple_of((me * SHARE + seg) * UNITS, UNITS)
-        return pltpu.make_async_copy(
-            x_ref.at[:, pl.ds(start, UNITS), :], buf.at[me, seg], recv_x.at[me, seg]
-        )
+        return buf.at[slot, :, pl.ds(pl.multiple_of(chunk * CHUNK, CHUNK), CHUNK), :]
+
+    own = pltpu.make_async_copy(
+        x_ref.at[:, pl.ds(pl.multiple_of(me * SHARE * UNITS, UNITS), SHARE * UNITS), :],
+        buf.at[me],
+        own_sem,
+    )
 
     def plane_copy(k, chunk):
         j = other(k)
         return pltpu.make_async_remote_copy(
             src_ref=part_of_x(j, chunk),
             dst_ref=place(me, chunk),
-            send_sem=send_plane.at[k - 1, chunk],
-            recv_sem=recv_x.at[me, chunk],
+            send_sem=send_x.at[0],
+            recv_sem=recv_plane.at[chunk],
             device_id=(base + j, tm),
             device_id_type=MESH,
         )
@@ -178,8 +178,8 @@
         return pltpu.make_async_remote_copy(
             src_ref=src,
             dst_ref=place(GROUP + j, chunk),
-            send_sem=send_z.at[k, chunk],
-            recv_sem=recv_x.at[GROUP + j, chunk],
+            send_sem=send_x.at[1],
+            recv_sem=recv_z.at[chunk],
             device_id=((rx + count + (j // 2 * 2 - 1) * GROUP) % count, tm),
             device_id_type=MESH,
         )
@@ -188,7 +188,7 @@
         return pltpu.make_async_remote_copy(
             src_ref=ref,
             dst_ref=ref,
-            send_sem=send_c.at[0, 0],
+            send_sem=send_c,
             recv_sem=sem,
             device_id=(rx, tm),
             device_id_type=MESH,
@@ -213,8 +213,7 @@
         greet(rx, (tm + step) % parts)
     for copy in tables:
         copy.start()
-    for seg in range(SHARE):
-        own_copy(seg).start()
+    own.start()
     pl.semaphore_wait(barrier, 2 + GROUP - 1 + parts - 1)
 
     for chunk in range(CHUNKS):
@@ -235,7 +234,7 @@
             pl.semaphore_signal(ready.at[2], 1, device_id=(to, tm), device_id_type=MESH)
 
     def pieces(slot, seg, comp):
-        rows = buf.at[slot, seg, comp]
+        rows = buf.at[slot, comp, pl.ds(pl.multiple_of(seg * UNITS, UNITS), UNITS), :]
         even = rows[pl.ds(0, BLOCKS, stride=2), :]
         odd = rows[pl.ds(1, BLOCKS, stride=2), :]
         return even, odd
@@ -289,18 +288,22 @@
 
         lax.fori_loop(0, 2, half_step, 0)
 
-    def arrived(slot, chunk):
-        received(place(slot, chunk), recv_x.at[slot, chunk]).wait_recv()
+    def arrived(slots, chunk, sem):
+        received(place(slots, chunk), sem.at[chunk]).wait_recv()
 
     def seg_step(step, carry):
         @pl.when(step < SHARE)
         def _():
             for part in range(SPLIT):
                 chunk = step * SPLIT + part
-                for k in range(1, GROUP):
-                    arrived(other(k), chunk)
+                arrived(slice(0, GROUP - 1), chunk, recv_plane)
+                for k in (2, 3, 1):
                     z_copy(k, chunk, place(other(k), chunk)).start()
-            own_copy(step).wait()
+
+            @pl.when(step == 0)
+            def _():
+                own.wait()
+
             window_spectra(range(0, 4), step, step)
             block_spectra(range(0, 3), step, step, 0)
 
@@ -308,8 +311,7 @@
         def _():
             seg = step - LAG_STEPS
             for part in range(SPLIT):
-                for slot in range(GROUP, 2 * GROUP):
-                    arrived(slot, seg * SPLIT + part)
+                arrived(slice(GROUP, 2 * GROUP), seg * SPLIT + part, recv_z)
             window_spectra(range(4, 6), seg, seg)
             block_spectra(range(6, 8), seg, seg, 4)
             correlate(seg, seg)
@@ -322,10 +324,10 @@
         j, to = other(k), (tm + step) % parts
         rows = pl.ds(half * HALF_ROWS, HALF_ROWS)
         return pltpu.make_async_remote_copy(
-            src_ref=ct.at[j, to, rows],
-            dst_ref=fin.at[tm, me, rows],
-            send_sem=send_c.at[half, min(k, 1)],
-            recv_sem=recv_c.at[half, min(k, 1)],
+            src_ref=ct.at[j * parts + to, rows],
+            dst_ref=fin.at[tm * GROUP + me, rows],
+            send_sem=send_c,
+            recv_sem=recv_c.at[0],
             device_id=(base + j, to),
             device_id_type=MESH,
         )
@@ -334,10 +336,10 @@
         to = (tm + step) % parts
         rows = pl.ds(half * HALF_ROWS, HALF_ROWS)
         return pltpu.make_async_remote_copy(
-            src_ref=ct.at[GROUP + i, to, rows],
-            dst_ref=low.at[tm, me, rows],
-            send_sem=send_c.at[half, 2],
-            recv_sem=recv_c.at[half, 2],
+            src_ref=ct.at[(GROUP + i) * parts + to, rows],
+            dst_ref=low.at[tm * GROUP + me, rows],
+            send_sem=send_c,
+            recv_sem=recv_c.at[1],
             device_id=(above + i, to),
             device_id_type=MESH,
         )
@@ -361,7 +363,7 @@
                             value = pltpu.roll(value, shift, 1)
                         tile = jnp.where(lane // LAG_DEV == off, value, tile)
                     rows = slice(half * HALF_ROWS, (half + 1) * HALF_ROWS)
-                    ct[slot, col * 4 + piece, rows] = tile
+                    ct[slot * parts + col * 4 + piece, rows] = tile
 
     steps = sorted(range(parts), key=lambda step: -min(step % 4, -step % 4))
 
@@ -388,23 +390,27 @@
     lax.fori_loop(SHARE // 2 + LAG_STEPS, SHARE + LAG_STEPS, seg_step, 0)
     send_lags(1)
 
-    fin[tm, me] = ct[me, tm]
+    fin[tm * GROUP + me] = ct[me * parts + tm]
     tables[2].wait()
-    for chunk in range(CHUNKS):
-        for k in range(GROUP):
-            if k:
-                plane_copy(k, chunk).wait_send()
-            z_copy(k, chunk, part_of_x(me, chunk)).wait_send()
-
-    for half in range(2):
-        rows = pl.ds(half * HALF_ROWS, HALF_ROWS)
-
-        @pl.when(me < 2)
-        def _():
-            received(low.at[:, :, rows], recv_c.at[half, 2]).wait_recv()
-
-        received(fin.at[:, : GROUP - 1, rows], recv_c.at[half, 1]).wait_recv()
-        received(fin.at[: parts - 1, 0, rows], recv_c.at[half, 0]).wait_recv()
+
+    def sent(ref, sem):
+        pltpu.make_async_remote_copy(
+            src_ref=ref,
+            dst_ref=ref,
+            send_sem=sem,
+            recv_sem=recv_c.at[0],
+            device_id=(rx, tm),
+            device_id_type=MESH,
+        ).wait_send()
+
+    sent(buf.at[: GROUP - 1], send_x.at[0])
+    sent(buf.at[:GROUP], send_x.at[1])
+
+    @pl.when(me < 2)
+    def _():
+        received(low, recv_c.at[1]).wait_recv()
+
+    received(fin.at[: parts * GROUP - 1], recv_c.at[0]).wait_recv()
 
     rows = parts * GROUP * 2 * SHARE
     lanes = lax.broadcasted_iota(jnp.int32, (rows, LANES), 1)
@@ -420,21 +426,7 @@
                 off * LAG_DEV : (off + 1) * LAG_DEV, col * LANES : (col + 1) * LANES
             ]
 
-    def sent(ref, sem):
-        pltpu.make_async_remote_copy(
-            src_ref=ref,
-            dst_ref=ref,
-            send_sem=sem,
-            recv_sem=recv_c.at[0, 0],
-            device_id=(rx, tm),
-            device_id_type=MESH,
-        ).wait_send()
-
-    for half in range(2):
-        rows = pl.ds(half * HALF_ROWS, HALF_ROWS)
-        sent(ct.at[0, : parts - 1, rows], send_c.at[half, 0])
-        sent(ct.at[: GROUP - 1, :, rows], send_c.at[half, 1])
-        sent(ct.at[GROUP : GROUP + 2, :, rows], send_c.at[half, 2])
+    sent(ct.at[: 6 * parts - 1], send_c)
 
 
 def per_device(planes, parts, signals):
@@ -447,23 +439,24 @@
         in_specs=[pl.BlockSpec(memory_space=pl.ANY)] * 4,
         out_specs=pl.BlockSpec(memory_space=pltpu.VMEM),
         scratch_shapes=[
-            vmem((2 * GROUP, SHARE, 2, UNITS, LANES), jnp.float32),
+            vmem((2 * GROUP, 2, SHARE * UNITS, LANES), jnp.float32),
             vmem((SHARE, 6 * BLOCKS, 2 * WINDOW), jnp.float32),
             vmem((SHARE, 6 * BLOCKS, 2 * WINDOW), jnp.float32),
             vmem((SHARE * 32, WINDOW), jnp.float32),
             vmem((2, SHARE * 32, LANES), jnp.float32),
-            vmem((6, parts, 8, LANES), jnp.float32),
-            vmem((parts, GROUP, 8, LANES), jnp.float32),
-            vmem((parts, GROUP, 8, LANES), jnp.float32),
+            vmem((6 * parts, 8, LANES), jnp.float32),
+            vmem((parts * GROUP, 8, LANES), jnp.float32),
+            vmem((parts * GROUP, 8, LANES), jnp.float32),
             vmem((2, WINDOW, WINDOW), jnp.bfloat16),
             vmem((2, WINDOW, LAGS), jnp.bfloat16),
             vmem((2, dop_rows, 2 * DOPK), jnp.bfloat16),
             dma((3,)),
-            dma((GROUP - 1, CHUNKS)),
-            dma((GROUP, CHUNKS)),
-            dma((2 * GROUP, CHUNKS)),
-            dma((2, 3)),
-            dma((2, 3)),
+            dma,
+            dma((2,)),
+            dma((CHUNKS,)),
+            dma((CHUNKS,)),
+            dma,
+            dma((2,)),
             pltpu.SemaphoreType.REGULAR((3,)),
         ],
         compiler_params=pltpu.CompilerParams(

time: 31 us -> 29.9 us (0.965)
  Pallas kernels: 30.2 us -> 29.1 us
    pallas_call x1, Pallas kernels: 30.2 us -> 29.1 us  [per_device(): pl.pallas_call(functools.partial(kernel, planes, parts), out_shape=jax.Sh...]
where the time goes in v7:
time: 29.9 us; the launch traced here: 29.8 us
  Pallas kernels  29.1 us (97%)
  other arithmetic  0.72 us (2%)
    pallas_call x1, Pallas kernels, per_device(): pl.pallas_call(functools.partial(kernel, planes, parts), out_shape=jax.Sh...  29.1 us
    mul x1, other arithmetic, per_device(): return out.reshape(LAG_DEV, 2, 1, OFFS, 1, DOPK) * jnp.float32(scale)  0.72 us

profile of v7, /device:TPU:1, one launch (start us, length us, event | category | flops | bytes accessed | tf_op | source)
XLA Modules:
  0.0 29.8 jit_solution(15710202194173049365)
XLA Ops:
  0.0 29.1 %ambiguity.1 = f32[512,128]{1,0:T(8,128)S(1)} custom-call(f32[2,512,128]{2,1,0:T(8,128)} %bitcast.2, bf16[2,512,512]{2,1,0:T(8,128)(2,1)} %constant.8.clone.fwd_hbm, bf16[2,512,256]{2,1,0:T(8,128)(2,1)} %constant.9.clone.inv_hbm, bf16[2,256,512]{2,1,0:T(8,128)(2,1)} %constant.10.clone.dop_hbm), custom_call_target="tpu_custom_call" | custom-call | tf_op jit(solution)/shard_map/ambiguity/pallas_call | solution.py:436
  29.1 0.7 %broadcast_multiply_fusion = f32[512,128]{1,0:T(8,128)} fusion(f32[512,128]{1,0:T(8,128)S(1)} %ambiguity.1), kind=kLoop, calls=%fused_computation | loop fusion | flops 65536 | bytes 524288 | tf_op jit(solution)/shard_map/mul | solution.py:473

commit v8 on v7

--- a/solution.py
+++ b/solution.py
@@ -23,7 +23,7 @@
 BLOCKS = SEG_LEN // 256
 LAG_DEV = 32
 HALF_ROWS = SHARE
-SPLIT = 1
+SPLIT = 2
 CHUNKS = SHARE * SPLIT
 LAG_STEPS = 3
 CHUNK = UNITS // SPLIT
@@ -99,14 +99,19 @@
 
 
 def row_sums(values):
-    index = lax.broadcasted_iota(jnp.int32, values[0].shape, 0)
+    index = lax.broadcasted_iota(jnp.int32, (8, LANES), 0)
+    zero = jnp.zeros((8, LANES), jnp.float32)
     step = 1
     while len(values) > 1:
         first = index // step % 2 == 0
-        values = [
-            jnp.where(first, a, b) + pltpu.roll(jnp.where(first, b, a), step, 0)
-            for a, b in zip(values[0::2], values[1::2])
-        ]
+        pairs = list(zip(values[0::2], values[1::2]))
+        values = []
+        for a, b in pairs:
+            if a is None and b is None:
+                values.append(None)
+                continue
+            a, b = zero if a is None else a, zero if b is None else b
+            values.append(jnp.where(first, a, b) + pltpu.roll(jnp.where(first, b, a), step, 0))
         step *= 2
     return values[0]
 
@@ -260,16 +265,25 @@
         store_spectra(mixed, ps, side, target * BLOCKS)
 
     order = [(slot, off, far) for slot, partners in enumerate(PAIRS) for off, far in partners]
-
-    def correlate(seg, side):
+    order.sort(key=lambda entry: entry[0] >= GROUP or entry[2] >= GROUP - 1)
+    inner = sum(slot < GROUP and far < GROUP - 1 for slot, _, far in order)
+
+    def correlate(seg, first, last):
         def half_step(half, carry):
             def part(ref, slot, index):
                 start = pl.multiple_of(index * (WINDOW // 2) + half * LANES, LANES)
-                return ref[side, slot * BLOCKS : (slot + 1) * BLOCKS, pl.ds(start, LANES)]
+                return ref[seg, slot * BLOCKS : (slot + 1) * BLOCKS, pl.ds(start, LANES)]
 
             for group in range(2):
+                places = range(group * 8, group * 8 + 8)
+                if not any(first <= place < last for place in places):
+                    continue
                 sums = []
-                for slot, _, far in order[group * 8 : group * 8 + 8]:
+                for place in places:
+                    if not first <= place < last:
+                        sums.append([None] * 4)
+                        continue
+                    slot, _, far = order[place]
                     q = [part(qs, slot, i) for i in range(4)]
                     p = [part(ps, far, i) for i in range(4)]
                     z = [
@@ -283,7 +297,10 @@
                 for i in range(4):
                     row = pl.multiple_of(seg * 32 + i // 2 * 16 + group * 8, 8)
                     lane = pl.multiple_of(i % 2 * (WINDOW // 2) + half * LANES, LANES)
-                    srow[pl.ds(row, 8), pl.ds(lane, LANES)] = row_sums([v[i] for v in sums])
+                    total = row_sums([v[i] for v in sums])
+                    if places[0] < first:
+                        total += srow[pl.ds(row, 8), pl.ds(lane, LANES)]
+                    srow[pl.ds(row, 8), pl.ds(lane, LANES)] = total
             return carry
 
         lax.fori_loop(0, 2, half_step, 0)
@@ -306,6 +323,7 @@
 
             window_spectra(range(0, 4), step, step)
             block_spectra(range(0, 3), step, step, 0)
+            correlate(step, 0, inner)
 
         @pl.when(step >= LAG_STEPS)
         def _():
@@ -314,7 +332,7 @@
                 arrived(slice(GROUP, 2 * GROUP), seg * SPLIT + part, recv_z)
             window_spectra(range(4, 6), seg, seg)
             block_spectra(range(6, 8), seg, seg, 4)
-            correlate(seg, seg)
+            correlate(seg, inner, len(order))
 
         return carry
 

time: 29.9 us -> 29.4 us (0.983)
  Pallas kernels: 29.1 us -> 28.6 us
    pallas_call x1, Pallas kernels: 29.1 us -> 28.6 us  [per_device(): pl.pallas_call(functools.partial(kernel, planes, parts), out_shape=jax.Sh...]
where the time goes in v8:
time: 29.4 us; the launch traced here: 29.3 us
  Pallas kernels  28.6 us (97%)
  other arithmetic  0.72 us (2%)
    pallas_call x1, Pallas kernels, per_device(): pl.pallas_call(functools.partial(kernel, planes, parts), out_shape=jax.Sh...  28.6 us
    mul x1, other arithmetic, per_device(): return out.reshape(LAG_DEV, 2, 1, OFFS, 1, DOPK) * jnp.float32(scale)  0.72 us

profile of v8, /device:TPU:1, one launch (start us, length us, event | category | flops | bytes accessed | tf_op | source)
XLA Modules:
  0.0 29.3 jit_solution(2911138727772285209)
XLA Ops:
  0.0 28.6 %ambiguity.1 = f32[512,128]{1,0:T(8,128)S(1)} custom-call(f32[2,512,128]{2,1,0:T(8,128)} %bitcast.2, bf16[2,512,512]{2,1,0:T(8,128)(2,1)} %constant.8.clone.fwd_hbm, bf16[2,512,256]{2,1,0:T(8,128)(2,1)} %constant.9.clone.inv_hbm, bf16[2,256,512]{2,1,0:T(8,128)(2,1)} %constant.10.clone.dop_hbm), custom_call_target="tpu_custom_call" | custom-call | tf_op jit(solution)/shard_map/ambiguity/pallas_call | solution.py:454
  28.6 0.7 %broadcast_multiply_fusion = f32[512,128]{1,0:T(8,128)} fusion(f32[512,128]{1,0:T(8,128)S(1)} %ambiguity.1), kind=kLoop, calls=%fused_computation | loop fusion | flops 65536 | bytes 524288 | tf_op jit(solution)/shard_map/mul | solution.py:491

commit v9 on v8

--- a/solution.py
+++ b/solution.py
@@ -25,7 +25,7 @@
 HALF_ROWS = SHARE
 SPLIT = 2
 CHUNKS = SHARE * SPLIT
-LAG_STEPS = 3
+LAG_STEPS = 4
 CHUNK = UNITS // SPLIT
 VMEM_LIMIT = 67043328 - 10800 * 1024
 
@@ -222,7 +222,7 @@
     pl.semaphore_wait(barrier, 2 + GROUP - 1 + parts - 1)
 
     for chunk in range(CHUNKS):
-        for k in (3, 2, 1):
+        for k in (3, 2, 1) if chunk % 2 else (2, 3, 1):
             plane_copy(k, chunk).start()
         z_copy(0, chunk, part_of_x(me, chunk)).start()
 
@@ -389,11 +389,10 @@
         rows = slice(half * SHARE * 16, (half + 1) * SHARE * 16)
         lags = product(srow[rows], inv[0], inv[1])
         corr[0, rows], corr[1, rows] = lags[:, :LANES], lags[:, LANES:]
-        tiles((4, 5), half)
+        tiles(range(6), half)
         for step in steps:
             for i in range(2):
                 low_copy(i, step, half).start()
-        tiles(range(4), half)
         for ks in ((3, 2), (1, 0)):
             for step in steps:
                 for k in ks:

time: 29.4 us -> 29.5 us (level)
  no operation moved by 1% of the time
where the time goes in v9:
time: 29.5 us; the launch traced here: 29.4 us
  Pallas kernels  28.7 us (97%)
  other arithmetic  0.72 us (2%)
    pallas_call x1, Pallas kernels, per_device(): pl.pallas_call(functools.partial(kernel, planes, parts), out_shape=jax.Sh...  28.7 us
    mul x1, other arithmetic, per_device(): return out.reshape(LAG_DEV, 2, 1, OFFS, 1, DOPK) * jnp.float32(scale)  0.72 us

profile of v9, /device:TPU:1, one launch (start us, length us, event | category | flops | bytes accessed | tf_op | source)
XLA Modules:
  0.0 29.4 jit_solution(4593981654478263674)
XLA Ops:
  0.0 28.7 %ambiguity.1 = f32[512,128]{1,0:T(8,128)S(1)} custom-call(f32[2,512,128]{2,1,0:T(8,128)} %bitcast.2, bf16[2,512,512]{2,1,0:T(8,128)(2,1)} %constant.8.clone.fwd_hbm, bf16[2,512,256]{2,1,0:T(8,128)(2,1)} %constant.9.clone.inv_hbm, bf16[2,256,512]{2,1,0:T(8,128)(2,1)} %constant.10.clone.dop_hbm), custom_call_target="tpu_custom_call" | custom-call | tf_op jit(solution)/shard_map/ambiguity/pallas_call | solution.py:453
  28.7 0.7 %broadcast_multiply_fusion = f32[512,128]{1,0:T(8,128)} fusion(f32[512,128]{1,0:T(8,128)S(1)} %ambiguity.1), kind=kLoop, calls=%fused_computation | loop fusion | flops 65536 | bytes 524288 | tf_op jit(solution)/shard_map/mul | solution.py:490

commit v10 on v8

--- a/solution.py
+++ b/solution.py
@@ -222,7 +222,7 @@
     pl.semaphore_wait(barrier, 2 + GROUP - 1 + parts - 1)
 
     for chunk in range(CHUNKS):
-        for k in (3, 2, 1):
+        for k in ((3, 2, 1) if chunk % 2 else (2, 3, 1)):
             plane_copy(k, chunk).start()
         z_copy(0, chunk, part_of_x(me, chunk)).start()
 

time: 29.4 us -> 29.4 us (level)
  no operation moved by 1% of the time
where the time goes in v10:
time: 29.4 us; the launch traced here: 29.3 us
  Pallas kernels  28.6 us (97%)
  other arithmetic  0.72 us (2%)
    pallas_call x1, Pallas kernels, per_device(): pl.pallas_call(functools.partial(kernel, planes, parts), out_shape=jax.Sh...  28.6 us
    mul x1, other arithmetic, per_device(): return out.reshape(LAG_DEV, 2, 1, OFFS, 1, DOPK) * jnp.float32(scale)  0.72 us

profile of v10, /device:TPU:1, one launch (start us, length us, event | category | flops | bytes accessed | tf_op | source)
XLA Modules:
  0.0 29.3 jit_solution(11302230571291412406)
XLA Ops:
  0.0 28.6 %ambiguity.1 = f32[512,128]{1,0:T(8,128)S(1)} custom-call(f32[2,512,128]{2,1,0:T(8,128)} %bitcast.2, bf16[2,512,512]{2,1,0:T(8,128)(2,1)} %constant.8.clone.fwd_hbm, bf16[2,512,256]{2,1,0:T(8,128)(2,1)} %constant.9.clone.inv_hbm, bf16[2,256,512]{2,1,0:T(8,128)(2,1)} %constant.10.clone.dop_hbm), custom_call_target="tpu_custom_call" | custom-call | tf_op jit(solution)/shard_map/ambiguity/pallas_call | solution.py:454
  28.6 0.7 %broadcast_multiply_fusion = f32[512,128]{1,0:T(8,128)} fusion(f32[512,128]{1,0:T(8,128)S(1)} %ambiguity.1), kind=kLoop, calls=%fused_computation | loop fusion | flops 65536 | bytes 524288 | tf_op jit(solution)/shard_map/mul | solution.py:491

commit v11 on v10

--- a/solution.py
+++ b/solution.py
@@ -314,7 +314,7 @@
             for part in range(SPLIT):
                 chunk = step * SPLIT + part
                 arrived(slice(0, GROUP - 1), chunk, recv_plane)
-                for k in (2, 3, 1):
+                for k in ((3, 2, 1) if part else (2, 3, 1)):
                     z_copy(k, chunk, place(other(k), chunk)).start()
 
             @pl.when(step == 0)

time: 29.4 us -> 29.4 us (level)
  no operation moved by 1% of the time
where the time goes in v11:
time: 29.4 us; the launch traced here: 29.3 us
  Pallas kernels  28.6 us (97%)
  other arithmetic  0.72 us (2%)
    pallas_call x1, Pallas kernels, per_device(): pl.pallas_call(functools.partial(kernel, planes, parts), out_shape=jax.Sh...  28.6 us
    mul x1, other arithmetic, per_device(): return out.reshape(LAG_DEV, 2, 1, OFFS, 1, DOPK) * jnp.float32(scale)  0.72 us

profile of v11, /device:TPU:1, one launch (start us, length us, event | category | flops | bytes accessed | tf_op | source)
XLA Modules:
  0.0 29.3 jit_solution(12284167644498670407)
XLA Ops:
  0.0 28.6 %ambiguity.1 = f32[512,128]{1,0:T(8,128)S(1)} custom-call(f32[2,512,128]{2,1,0:T(8,128)} %bitcast.2, bf16[2,512,512]{2,1,0:T(8,128)(2,1)} %constant.8.clone.fwd_hbm, bf16[2,512,256]{2,1,0:T(8,128)(2,1)} %constant.9.clone.inv_hbm, bf16[2,256,512]{2,1,0:T(8,128)(2,1)} %constant.10.clone.dop_hbm), custom_call_target="tpu_custom_call" | custom-call | tf_op jit(solution)/shard_map/ambiguity/pallas_call | solution.py:454
  28.6 0.7 %broadcast_multiply_fusion = f32[512,128]{1,0:T(8,128)} fusion(f32[512,128]{1,0:T(8,128)S(1)} %ambiguity.1), kind=kLoop, calls=%fused_computation | loop fusion | flops 65536 | bytes 524288 | tf_op jit(solution)/shard_map/mul | solution.py:491
